TPU v7x, 32 devices: a whole 2x2x4 slice. The times are simulated.
32 devices in a mesh: dp: 8 (over z, y), tensor: 4 (over x, core).
Axes of the slice: x: 2, y: 2, z: 4, core: 2. Of those that a mesh axis runs over, the one named last changes fastest.
Arguments:
- tokens: bfloat16 [16384, 768], P('dp'), may hold values from -6 to 6
- cotangent: bfloat16 [16384, 768], P('dp'), may hold values from -6 to 6
- key_lengths: int32 [32], P('dp'), may hold values from 256 to 512, as said below
- slot_counts: int32 [8], P('dp'), may hold values from 1 to 4, as said below
- w_query: bfloat16 [768, 768], P(None, 'tensor'), may hold values from -0.4375 to 0.4375
- b_query: bfloat16 [768], P('tensor'), may hold values from -3 to 3
- w_key: bfloat16 [768, 768], P(None, 'tensor'), may hold values from -0.21875 to 0.21875
- w_value: bfloat16 [768, 768], P(None, 'tensor'), may hold values from -0.21875 to 0.21875
- b_value: bfloat16 [768], P('tensor'), may hold values from -3 to 3
- w_out: bfloat16 [768, 768], P('tensor'), may hold values from -0.875 to 0.875
- b_out: bfloat16 [768], replicated, may hold values from -2 to 2
- attn_gain: bfloat16 [768], replicated, may hold values from 0.5 to 1.5
- attn_shift: bfloat16 [768], replicated, may hold values from -2 to 2
- w_up: bfloat16 [768, 3072], P(None, 'tensor'), may hold values from -0.21875 to 0.21875
- b_up: bfloat16 [3072], P('tensor'), may hold values from -3 to 3
- w_down: bfloat16 [3072, 768], P('tensor'), may hold values from -0.109375 to 0.109375
- b_down: bfloat16 [768], replicated, may hold values from -2 to 2
- ffn_gain: bfloat16 [768], replicated, may hold values from 0.5 to 1.5
- ffn_shift: bfloat16 [768], replicated, may hold values from -2 to 2
Outputs:
- layer_out: bfloat16 [16384, 768], P('dp')
- grad_tokens: bfloat16 [16384, 768], P('dp')
- grad_w_query: float32 [768, 768], P(None, 'tensor')
- grad_b_query: float32 [768], P('tensor')
- grad_w_key: float32 [768, 768], P(None, 'tensor')
- grad_w_value: float32 [768, 768], P(None, 'tensor')
- grad_b_value: float32 [768], P('tensor')
- grad_w_out: float32 [768, 768], P('tensor')
- grad_b_out: float32 [768], replicated
- grad_attn_gain: float32 [768], replicated
- grad_attn_shift: float32 [768], replicated
- grad_w_up: float32 [768, 3072], P(None, 'tensor')
- grad_b_up: float32 [3072], P('tensor')
- grad_w_down: float32 [3072, 768], P('tensor')
- grad_b_down: float32 [768], replicated
- grad_ffn_gain: float32 [768], replicated
- grad_ffn_shift: float32 [768], replicated
Inputs may be any that keep to these rules, and one draw needn't show every extreme that they name: `key_lengths`: each slot's key length is between 256 and 512; the first slot's is 512. `slot_counts`: each group has 1 to 4 live slots; group 0 has 4.
All inputs are finite; a program needn't handle non-finite values.
Results may differ from a plain program's by a relative error of at most 0.019.
Values may be sent and summed in bfloat16 or wider, within the bound.
A program may use at most 128 MiB of HBM per device.

v0:
```python
import jax
import jax.numpy as jnp
from jax import lax
from jax.sharding import PartitionSpec as P

HD = 64
SEQ = 512


def normalize(hidden, gain, shift):
    center = hidden - jnp.mean(hidden, -1, keepdims=True)
    inv_std = lax.rsqrt(jnp.mean(center * center, -1, keepdims=True) + 1e-05)
    normed = center * inv_std
    return (normed * gain + shift, normed, inv_std)


def norm_back(grad_normed, normed, inv_std):
    return inv_std * (
        grad_normed
        - jnp.mean(grad_normed, -1, keepdims=True)
        - normed * jnp.mean(grad_normed * normed, -1, keepdims=True)
    )


def gelu_exact(values):
    return jax.nn.gelu(values, approximate=False)


def column_sum(matrix):
    return jnp.sum(matrix.astype(jnp.float32), 0)


def run_slot(slot_index, live_factor, tokens, cotangent, key_lengths, params):
    (
        w_query,
        b_query,
        w_key,
        w_value,
        b_value,
        w_out,
        b_out,
        attn_gain,
        attn_shift,
        w_up,
        b_up,
        w_down,
        b_down,
        ffn_gain,
        ffn_shift,
    ) = params
    f32 = jnp.float32
    bf16 = jnp.bfloat16
    heads_local = w_query.shape[1] // HD
    head_shape = (SEQ, heads_local, HD)
    row_start = slot_index * SEQ
    tok_rows = lax.dynamic_slice_in_dim(tokens, row_start, SEQ, 0)
    grad_rows = lax.dynamic_slice_in_dim(cotangent, row_start, SEQ, 0).astype(f32) * live_factor
    length = key_lengths[slot_index]
    query_rows = (jnp.dot(tok_rows, w_query, preferred_element_type=f32) + b_query).astype(bf16)
    key_rows = jnp.dot(tok_rows, w_key, preferred_element_type=f32).astype(bf16)
    value_rows = (jnp.dot(tok_rows, w_value, preferred_element_type=f32) + b_value).astype(bf16)
    query_heads = query_rows.reshape(head_shape)
    key_heads = key_rows.reshape(head_shape)
    value_heads = value_rows.reshape(head_shape)
    valid_keys = (jnp.arange(SEQ) < length)[None, None, :]

    def masked_scores():
        scores = (
            jnp.einsum("qhd,khd->hqk", query_heads, key_heads, preferred_element_type=f32) * 0.125
        )
        return jnp.where(valid_keys, scores, -1e30)

    scores = masked_scores()
    top_score = jnp.max(scores, -1, keepdims=True)
    shifted_exp = jnp.exp(scores - top_score)
    totals = jnp.sum(shifted_exp, -1, keepdims=True)
    attn_probs = shifted_exp / totals
    log_total = top_score + jnp.log(totals)
    probs_low = attn_probs.astype(bf16)
    context = jnp.einsum("hqk,khd->qhd", probs_low, value_heads, preferred_element_type=f32)
    context = context.reshape(SEQ, -1).astype(bf16)
    attn_out = lax.psum(jnp.dot(context, w_out, preferred_element_type=f32), "tensor") + b_out
    resid_one = tok_rows.astype(f32) + attn_out
    first_out, first_normed, first_inv = normalize(resid_one, attn_gain, attn_shift)
    first_low = first_out.astype(bf16)
    hidden_pre = jnp.dot(first_low, w_up, preferred_element_type=f32) + b_up
    hidden_act, gelu_pull = jax.vjp(gelu_exact, hidden_pre)
    hidden_low = hidden_act.astype(bf16)
    ffn_out = (
        lax.psum(
            jnp.dot(hidden_low, w_down, preferred_element_type=f32).astype(jnp.bfloat16), "tensor"
        ).astype(jnp.float32)
        + b_down
    )
    resid_two = first_out + ffn_out
    layer_rows, second_normed, second_inv = normalize(resid_two, ffn_gain, ffn_shift)
    grad_ffn_gain = jnp.sum(grad_rows * second_normed, 0)
    grad_ffn_shift = jnp.sum(grad_rows, 0)
    grad_resid_two = norm_back(grad_rows * ffn_gain, second_normed, second_inv)
    grad_ffn_low = grad_resid_two.astype(bf16)
    grad_b_down = column_sum(grad_ffn_low)
    grad_w_down = jnp.einsum("rf,rd->fd", hidden_low, grad_ffn_low, preferred_element_type=f32)
    grad_hidden = jnp.einsum("rd,fd->rf", grad_ffn_low, w_down, preferred_element_type=f32)
    grad_pre_low = gelu_pull(grad_hidden)[0].astype(bf16)
    grad_b_up = column_sum(grad_pre_low)
    grad_w_up = jnp.einsum("rd,rf->df", first_low, grad_pre_low, preferred_element_type=f32)
    up_back = jnp.einsum("rf,df->rd", grad_pre_low, w_up, preferred_element_type=f32)
    grad_first = grad_resid_two + lax.psum(up_back.astype(jnp.bfloat16), "tensor").astype(
        jnp.float32
    )
    grad_attn_gain = jnp.sum(grad_first * first_normed, 0)
    grad_attn_shift = jnp.sum(grad_first, 0)
    grad_resid_one = norm_back(grad_first * attn_gain, first_normed, first_inv)
    grad_attn_low = grad_resid_one.astype(bf16)
    grad_b_out = column_sum(grad_attn_low)
    grad_w_out = jnp.einsum("rc,rd->cd", context, grad_attn_low, preferred_element_type=f32)
    grad_context = jnp.einsum("rd,cd->rc", grad_attn_low, w_out, preferred_element_type=f32)
    grad_context = grad_context.astype(bf16).reshape(head_shape)
    kept_probs = jnp.exp(masked_scores() - log_total)
    grad_probs = jnp.einsum("qhd,khd->hqk", grad_context, value_heads, preferred_element_type=f32)
    grad_scores = kept_probs * (grad_probs - jnp.sum(grad_probs * kept_probs, -1, keepdims=True))
    grad_scores = grad_scores.astype(bf16)
    grad_query = (
        jnp.einsum("hqk,khd->qhd", grad_scores, key_heads, preferred_element_type=f32) * 0.125
    )
    grad_query = grad_query.reshape(SEQ, -1).astype(bf16)
    grad_key = (
        jnp.einsum("hqk,qhd->khd", grad_scores, query_heads, preferred_element_type=f32) * 0.125
    )
    grad_key = grad_key.reshape(SEQ, -1).astype(bf16)
    grad_value = jnp.einsum(
        "hqk,qhd->khd", kept_probs.astype(bf16), grad_context, preferred_element_type=f32
    )
    grad_value = grad_value.reshape(SEQ, -1).astype(bf16)
    grad_b_query = column_sum(grad_query)
    grad_b_value = column_sum(grad_value)
    grad_w_query = jnp.einsum("rd,rc->dc", tok_rows, grad_query, preferred_element_type=f32)
    grad_w_key = jnp.einsum("rd,rc->dc", tok_rows, grad_key, preferred_element_type=f32)
    grad_w_value = jnp.einsum("rd,rc->dc", tok_rows, grad_value, preferred_element_type=f32)
    input_back = (
        jnp.einsum("rc,dc->rd", grad_query, w_query, preferred_element_type=f32)
        + jnp.einsum("rc,dc->rd", grad_key, w_key, preferred_element_type=f32)
        + jnp.einsum("rc,dc->rd", grad_value, w_value, preferred_element_type=f32)
    )
    grad_tok = grad_resid_one + lax.psum(input_back.astype(jnp.bfloat16), "tensor").astype(
        jnp.float32
    )
    layer_low = (layer_rows * live_factor).astype(bf16)
    grad_low = grad_tok.astype(bf16)
    grads = (
        grad_w_query,
        grad_b_query,
        grad_w_key,
        grad_w_value,
        grad_b_value,
        grad_w_out,
        grad_b_out,
        grad_attn_gain,
        grad_attn_shift,
        grad_w_up,
        grad_b_up,
        grad_w_down,
        grad_b_down,
        grad_ffn_gain,
        grad_ffn_shift,
    )
    return (layer_low, grad_low, grads)


def place_slot(carry, slot_index, layer_low, grad_low, grads):
    out_buffer, grad_buffer, totals = carry
    row_start = slot_index * SEQ
    out_buffer = lax.dynamic_update_slice_in_dim(out_buffer, layer_low, row_start, 0)
    grad_buffer = lax.dynamic_update_slice_in_dim(grad_buffer, grad_low, row_start, 0)
    totals = jax.tree.map(jnp.add, totals, grads)
    return (out_buffer, grad_buffer, totals)


def per_device(
    tokens,
    cotangent,
    key_lengths,
    slot_counts,
    w_query,
    b_query,
    w_key,
    w_value,
    b_value,
    w_out,
    b_out,
    attn_gain,
    attn_shift,
    w_up,
    b_up,
    w_down,
    b_down,
    ffn_gain,
    ffn_shift,
):
    params = (
        w_query,
        b_query,
        w_key,
        w_value,
        b_value,
        w_out,
        b_out,
        attn_gain,
        attn_shift,
        w_up,
        b_up,
        w_down,
        b_down,
        ffn_gain,
        ffn_shift,
    )
    slot_total = key_lengths.shape[0]
    live_count = slot_counts[0]
    zero_grads = tuple((jnp.zeros(weight.shape, jnp.float32) for weight in params))
    state = (jnp.zeros_like(tokens), jnp.zeros_like(tokens), zero_grads)

    def masked_step(slot_index, carry):
        live_factor = (slot_index < live_count).astype(jnp.float32)
        layer_low, grad_low, grads = run_slot(
            slot_index, live_factor, tokens, cotangent, key_lengths, params
        )
        return place_slot(carry, slot_index, layer_low, grad_low, grads)

    state = lax.fori_loop(0, slot_total, masked_step, state)
    layer_out, grad_tokens, totals = state
    summed = lax.psum(totals, "dp")
    return (
        layer_out,
        grad_tokens,
        summed[0],
        summed[1],
        summed[2],
        summed[3],
        summed[4],
        summed[5],
        summed[6],
        summed[7],
        summed[8],
        summed[9],
        summed[10],
        summed[11],
        summed[12],
        summed[13],
        summed[14],
    )


def solution(mesh):
    placed = (
        P("dp", None),
        P("dp", None),
        P("dp"),
        P("dp"),
        P(None, "tensor"),
        P("tensor"),
        P(None, "tensor"),
        P(None, "tensor"),
        P("tensor"),
        P("tensor", None),
        P(),
        P(),
        P(),
        P(None, "tensor"),
        P("tensor"),
        P("tensor", None),
        P(),
        P(),
        P(),
    )
    return jax.shard_map(
        per_device,
        mesh=mesh,
        in_specs=placed,
        out_specs=(
            P("dp", None),
            P("dp", None),
            P(None, "tensor"),
            P("tensor"),
            P(None, "tensor"),
            P(None, "tensor"),
            P("tensor"),
            P("tensor", None),
            P(),
            P(),
            P(),
            P(None, "tensor"),
            P("tensor"),
            P("tensor", None),
            P(),
            P(),
            P(),
        ),
        check_vma=False,
    )
```

profile of v0, /device:TPU:0, one launch (start us, length us, event | category | flops | bytes accessed | tf_op | source)
XLA Modules:
  0.0 1067.4 jit_solution(7840052050258792703)
XLA Ops:
  11.9 801.4 %while.46 = (s32[]{:T(128)}, bf16[2048,768]{1,0:T(8,128)(2,1)}, bf16[2048,768]{1,0:T(8,128)(2,1)}, f32[768,192]{0,1:T(8,128)}, f32[192]{0:T(256)}, /*index=5*/f3...) while((s32[]{:T(128)}, bf16[2048,768]{1,0:T(8,128)(2,1)}, ...), condition=%wide.region_25.26_spmd.clone, body=%wide.region_0.25_spmd.clone.sunk | while | flops 6128281088 | bytes 279827168 | solution.py:229
  26.9 43.6 %all-reduce.10.cloned.1.call-done = f32[512,768]{1,0:T(8,128)} async-done(((f32[512,768]{1,0:T(8,128)}), f32[512,768]{1,0:T(8,128)}) %all-reduce.10.cloned.1.call-update) | async-done | bytes 1572880 | tf_op jit(solution)/shard_map/while/body/eval_jaxpr/psum | solution.py:82
  74.2 5.4 multiply_convert_fusion.5
  83.1 34.4 %all-reduce.12.cloned.1.call-done = bf16[512,768]{1,0:T(8,128)(2,1)} async-done(((bf16[512,768]{1,0:T(8,128)(2,1)}), bf16[512,768]{1,0:T(8,128)(2,1)}) %all-reduce.12.cloned.1.call-update) | async-done | bytes 786448 | tf_op jit(solution)/shard_map/while/body/eval_jaxpr/psum | solution.py:90
  135.9 26.8 %all-reduce.14.cloned.1.call-done = bf16[512,768]{1,0:T(8,128)(2,1)} async-done(((bf16[512,768]{1,0:T(8,128)(2,1)}), bf16[512,768]{1,0:T(8,128)(2,1)}) %all-reduce.14.cloned.1.call-update) | async-done | bytes 786448 | tf_op jit(solution)/shard_map/while/body/eval_jaxpr/psum | solution.py:108
  184.0 28.0 %all-reduce.16.cloned.1.call-done = bf16[512,768]{1,0:T(8,128)(2,1)} async-done(((bf16[512,768]{1,0:T(8,128)(2,1)}), bf16[512,768]{1,0:T(8,128)(2,1)}) %all-reduce.16.cloned.1.call-update) | async-done | bytes 786448 | tf_op jit(solution)/shard_map/while/body/eval_jaxpr/psum | solution.py:145
  229.3 40.9 %all-reduce.10.cloned.1.call-done = f32[512,768]{1,0:T(8,128)} async-done(((f32[512,768]{1,0:T(8,128)}), f32[512,768]{1,0:T(8,128)}) %all-reduce.10.cloned.1.call-update) | async-done | bytes 1572880 | tf_op jit(solution)/shard_map/while/body/eval_jaxpr/psum | solution.py:82
  273.9 5.4 multiply_convert_fusion.5
  282.8 34.4 %all-reduce.12.cloned.1.call-done = bf16[512,768]{1,0:T(8,128)(2,1)} async-done(((bf16[512,768]{1,0:T(8,128)(2,1)}), bf16[512,768]{1,0:T(8,128)(2,1)}) %all-reduce.12.cloned.1.call-update) | async-done | bytes 786448 | tf_op jit(solution)/shard_map/while/body/eval_jaxpr/psum | solution.py:90
  338.0 24.3 %all-reduce.14.cloned.1.call-done = bf16[512,768]{1,0:T(8,128)(2,1)} async-done(((bf16[512,768]{1,0:T(8,128)(2,1)}), bf16[512,768]{1,0:T(8,128)(2,1)}) %all-reduce.14.cloned.1.call-update) | async-done | bytes 786448 | tf_op jit(solution)/shard_map/while/body/eval_jaxpr/psum | solution.py:108
  385.0 26.7 %all-reduce.16.cloned.1.call-done = bf16[512,768]{1,0:T(8,128)(2,1)} async-done(((bf16[512,768]{1,0:T(8,128)(2,1)}), bf16[512,768]{1,0:T(8,128)(2,1)}) %all-reduce.16.cloned.1.call-update) | async-done | bytes 786448 | tf_op jit(solution)/shard_map/while/body/eval_jaxpr/psum | solution.py:145
  429.0 40.9 %all-reduce.10.cloned.1.call-done = f32[512,768]{1,0:T(8,128)} async-done(((f32[512,768]{1,0:T(8,128)}), f32[512,768]{1,0:T(8,128)}) %all-reduce.10.cloned.1.call-update) | async-done | bytes 1572880 | tf_op jit(solution)/shard_map/while/body/eval_jaxpr/psum | solution.py:82
  473.6 5.4 multiply_convert_fusion.5
  482.4 34.5 %all-reduce.12.cloned.1.call-done = bf16[512,768]{1,0:T(8,128)(2,1)} async-done(((bf16[512,768]{1,0:T(8,128)(2,1)}), bf16[512,768]{1,0:T(8,128)(2,1)}) %all-reduce.12.cloned.1.call-update) | async-done | bytes 786448 | tf_op jit(solution)/shard_map/while/body/eval_jaxpr/psum | solution.py:90
  526.9 4.9 select_add_fusion.21
  537.7 24.3 %all-reduce.14.cloned.1.call-done = bf16[512,768]{1,0:T(8,128)(2,1)} async-done(((bf16[512,768]{1,0:T(8,128)(2,1)}), bf16[512,768]{1,0:T(8,128)(2,1)}) %all-reduce.14.cloned.1.call-update) | async-done | bytes 786448 | tf_op jit(solution)/shard_map/while/body/eval_jaxpr/psum | solution.py:108
  584.7 26.7 %all-reduce.16.cloned.1.call-done = bf16[512,768]{1,0:T(8,128)(2,1)} async-done(((bf16[512,768]{1,0:T(8,128)(2,1)}), bf16[512,768]{1,0:T(8,128)(2,1)}) %all-reduce.16.cloned.1.call-update) | async-done | bytes 786448 | tf_op jit(solution)/shard_map/while/body/eval_jaxpr/psum | solution.py:145
  628.7 40.9 %all-reduce.10.cloned.1.call-done = f32[512,768]{1,0:T(8,128)} async-done(((f32[512,768]{1,0:T(8,128)}), f32[512,768]{1,0:T(8,128)}) %all-reduce.10.cloned.1.call-update) | async-done | bytes 1572880 | tf_op jit(solution)/shard_map/while/body/eval_jaxpr/psum | solution.py:82
  673.3 5.4 multiply_convert_fusion.5
  682.1 34.5 %all-reduce.12.cloned.1.call-done = bf16[512,768]{1,0:T(8,128)(2,1)} async-done(((bf16[512,768]{1,0:T(8,128)(2,1)}), bf16[512,768]{1,0:T(8,128)(2,1)}) %all-reduce.12.cloned.1.call-update) | async-done | bytes 786448 | tf_op jit(solution)/shard_map/while/body/eval_jaxpr/psum | solution.py:90
  737.4 24.3 %all-reduce.14.cloned.1.call-done = bf16[512,768]{1,0:T(8,128)(2,1)} async-done(((bf16[512,768]{1,0:T(8,128)(2,1)}), bf16[512,768]{1,0:T(8,128)(2,1)}) %all-reduce.14.cloned.1.call-update) | async-done | bytes 786448 | tf_op jit(solution)/shard_map/while/body/eval_jaxpr/psum | solution.py:108
  784.4 26.7 %all-reduce.16.cloned.1.call-done = bf16[512,768]{1,0:T(8,128)(2,1)} async-done(((bf16[512,768]{1,0:T(8,128)(2,1)}), bf16[512,768]{1,0:T(8,128)(2,1)}) %all-reduce.16.cloned.1.call-update) | async-done | bytes 786448 | tf_op jit(solution)/shard_map/while/body/eval_jaxpr/psum | solution.py:145
  814.2 39.6 %all-reduce = (f32[192]{0:T(256)}, f32[192]{0:T(256)}, f32[768]{0:T(1024)}, f32[768]{0:T(1024)}, f32[768]{0:T(1024)}, /*index=5*/f32[768]{0:T(1024)}, f32[768]{0:T(1024)}, f32[768]{0:T(1024)}, f32[768]{0:T(1024)}) all-reduce(f32[192]{0:T(256)S(1)} %copy-done.65, f32[192]{0:T(256)S(1)} %copy-done.68, ...), channel_id=1, replica_groups=mesh['dp'=8,'tensor'=4] {'dp'}, use_global_device_ids=true, to_apply=%region_27.28 | all-reduce | flops 5760 | bytes 46080 | tf_op jit(solution)/shard_map/psum | solution.py:231
  853.8 198.1 %all-reduce.8.cloned.1.call-done = (f32[768,192]{0,1:T(8,128)}, f32[768,192]{0,1:T(8,128)}, f32[768,192]{0,1:T(8,128)}, f32[192,768]{1,0:T(8,128)}, f32[768,768]{1,0:T(8,128)}, /*index=5*/f32[768,768]{1,0:T(8,128)}) async-done(((f32[768,192]{0,1:T(8,128)}, f32[768,192]{0,1:T(8,128)}, f32[768,192]{0,1:T(8,128)}, f32[192,768]{1,0:T(8,128)}, f32[768,768]{1,0:T(8,128)}, /*index=5*/f32[768,768]{1,0:T(8,128)}), ...) | async-done | bytes 7077904 | tf_op jit(solution)/shard_map/psum | solution.py:231
  (828 shorter events, 269.8 us)
Async XLA Ops:
  11.9 58.6 %all-reduce.10.cloned.1.call-start = ((), (), s32[]{:S(2)}) async-start(), calls=%async_computation.1 | async-start | bytes 3145728 | tf_op jit(solution)/shard_map/while/body/eval_jaxpr/psum | solution.py:82
  24.8 92.7 %all-reduce.12.cloned.1.call-start = ((), (), s32[]{:S(2)}) async-start(), calls=%async_computation.2 | async-start | bytes 1572864 | tf_op jit(solution)/shard_map/while/body/eval_jaxpr/psum | solution.py:90
  82.3 80.3 %all-reduce.14.cloned.1.call-start = ((), (), s32[]{:S(2)}) async-start(), calls=%async_computation.3 | async-start | bytes 1572864 | tf_op jit(solution)/shard_map/while/body/eval_jaxpr/psum | solution.py:108
  127.4 84.6 %all-reduce.16.cloned.1.call-start = ((), (), s32[]{:S(2)}) async-start(), calls=%async_computation.4 | async-start | bytes 1572864 | tf_op jit(solution)/shard_map/while/body/eval_jaxpr/psum | solution.py:145
  182.6 31.6 %copy-start.13 = (f32[768,192]{0,1:T(8,128)}, f32[768,192]{0,1:T(8,128)S(1)}, u32[]{:S(2)}) copy-start(f32[768,192]{0,1:T(8,128)S(1)} %convolution_add_fusion.11) | copy-start | bytes 1769476 | tf_op jit(solution)/shard_map/while
  182.7 31.5 %copy-start.42 = (f32[768]{0:T(1024)}, f32[768]{0:T(1024)S(1)}, u32[]{:S(2)}) copy-start(f32[768]{0:T(1024)S(1)} %get-tuple-element.1255) | copy-start | bytes 9220 | tf_op jit(solution)/shard_map/while
  182.7 31.5 %copy-start.57 = (f32[768]{0:T(1024)}, f32[768]{0:T(1024)S(1)}, u32[]{:S(2)}) copy-start(f32[768]{0:T(1024)S(1)} %get-tuple-element.1251) | copy-start | bytes 9220 | tf_op jit(solution)/shard_map/while
  182.8 31.4 %copy-start.51 = (f32[768]{0:T(1024)}, f32[768]{0:T(1024)S(1)}, u32[]{:S(2)}) copy-start(f32[768]{0:T(1024)S(1)} %get-tuple-element.1249) | copy-start | bytes 9220 | tf_op jit(solution)/shard_map/while
  182.8 31.4 %copy-start.54 = (f32[768]{0:T(1024)}, f32[768]{0:T(1024)S(1)}, u32[]{:S(2)}) copy-start(f32[768]{0:T(1024)S(1)} %get-tuple-element.1250) | copy-start | bytes 9220 | tf_op jit(solution)/shard_map/while
  182.8 31.4 %copy-start.64 = (f32[192]{0:T(256)}, f32[192]{0:T(256)S(1)}, u32[]{:S(2)}) copy-start(f32[192]{0:T(256)S(1)} %get-tuple-element.1244) | copy-start | bytes 2308 | tf_op jit(solution)/shard_map/while
  182.8 31.4 %copy-start.67 = (f32[192]{0:T(256)}, f32[192]{0:T(256)S(1)}, u32[]{:S(2)}) copy-start(f32[192]{0:T(256)S(1)} %get-tuple-element.1247) | copy-start | bytes 2308 | tf_op jit(solution)/shard_map/while
  214.3 55.9 %all-reduce.10.cloned.1.call-start = ((), (), s32[]{:S(2)}) async-start(), calls=%async_computation.1 | async-start | bytes 3145728 | tf_op jit(solution)/shard_map/while/body/eval_jaxpr/psum | solution.py:82
  227.2 90.0 %all-reduce.12.cloned.1.call-start = ((), (), s32[]{:S(2)}) async-start(), calls=%async_computation.2 | async-start | bytes 1572864 | tf_op jit(solution)/shard_map/while/body/eval_jaxpr/psum | solution.py:90
  282.0 80.3 %all-reduce.14.cloned.1.call-start = ((), (), s32[]{:S(2)}) async-start(), calls=%async_computation.3 | async-start | bytes 1572864 | tf_op jit(solution)/shard_map/while/body/eval_jaxpr/psum | solution.py:108
  327.1 84.6 %all-reduce.16.cloned.1.call-start = ((), (), s32[]{:S(2)}) async-start(), calls=%async_computation.4 | async-start | bytes 1572864 | tf_op jit(solution)/shard_map/while/body/eval_jaxpr/psum | solution.py:145
  413.9 55.9 %all-reduce.10.cloned.1.call-start = ((), (), s32[]{:S(2)}) async-start(), calls=%async_computation.1 | async-start | bytes 3145728 | tf_op jit(solution)/shard_map/while/body/eval_jaxpr/psum | solution.py:82
  426.8 90.0 %all-reduce.12.cloned.1.call-start = ((), (), s32[]{:S(2)}) async-start(), calls=%async_computation.2 | async-start | bytes 1572864 | tf_op jit(solution)/shard_map/while/body/eval_jaxpr/psum | solution.py:90
  481.6 80.4 %all-reduce.14.cloned.1.call-start = ((), (), s32[]{:S(2)}) async-start(), calls=%async_computation.3 | async-start | bytes 1572864 | tf_op jit(solution)/shard_map/while/body/eval_jaxpr/psum | solution.py:108
  526.8 84.6 %all-reduce.16.cloned.1.call-start = ((), (), s32[]{:S(2)}) async-start(), calls=%async_computation.4 | async-start | bytes 1572864 | tf_op jit(solution)/shard_map/while/body/eval_jaxpr/psum | solution.py:145
  613.6 55.9 %all-reduce.10.cloned.1.call-start = ((), (), s32[]{:S(2)}) async-start(), calls=%async_computation.1 | async-start | bytes 3145728 | tf_op jit(solution)/shard_map/while/body/eval_jaxpr/psum | solution.py:82
  626.6 90.0 %all-reduce.12.cloned.1.call-start = ((), (), s32[]{:S(2)}) async-start(), calls=%async_computation.2 | async-start | bytes 1572864 | tf_op jit(solution)/shard_map/while/body/eval_jaxpr/psum | solution.py:90
  681.3 80.4 %all-reduce.14.cloned.1.call-start = ((), (), s32[]{:S(2)}) async-start(), calls=%async_computation.3 | async-start | bytes 1572864 | tf_op jit(solution)/shard_map/while/body/eval_jaxpr/psum | solution.py:108
  726.6 84.6 %all-reduce.16.cloned.1.call-start = ((), (), s32[]{:S(2)}) async-start(), calls=%async_computation.4 | async-start | bytes 1572864 | tf_op jit(solution)/shard_map/while/body/eval_jaxpr/psum | solution.py:145
  813.3 238.5 %all-reduce.8.cloned.1.call-start = ((), (), s32[]{:S(2)}) async-start(), calls=%async_computation | async-start | bytes 14155776 | tf_op jit(solution)/shard_map/psum | solution.py:231
  (255 other events, 1201.6 us)
Sparse Core Ops, SparseCore 0:
  24.9 45.5 all-reduce.9
  82.4 35.0 all-reduce.11
  127.6 35.0 all-reduce.13
  176.9 35.0 all-reduce.15
  227.3 42.8 all-reduce.9
  282.1 35.0 all-reduce.11
  327.2 35.0 all-reduce.13
  376.6 35.0 all-reduce.15
  427.0 42.8 all-reduce.9
  481.8 35.0 all-reduce.11
  527.0 35.0 all-reduce.13
  576.3 35.0 all-reduce.15
  626.7 42.8 all-reduce.9
  681.5 35.0 all-reduce.11
  726.7 35.0 all-reduce.13
  776.0 35.0 all-reduce.15
Sparse Core Ops, SparseCore 1:
  820.0 231.8 all-reduce.7
where the time goes:
time: 1070 us
  waiting for transfers between devices  711 us (66%)
  matrix products  165 us (15%)
  other arithmetic  80.9 us (8%)
  local copies, waits for them, and re-layouts  49 us (5%)
  blocking collectives  39.6 us (4%)
  between operations  15.4 us (1%)
    psum x1, waiting for transfers between devices, per_device(): summed = lax.psum(totals, 'dp')  198 us
    psum x4, waiting for transfers between devices, run_slot(): lax.psum(jnp.dot(context, w_out, preferred_element_type=f32), 'tensor')  166 us
    psum x4, waiting for transfers between devices, run_slot(): lax.psum(jnp.dot(hidden_low, w_down, preferred_element_type=f32).astype(j...  138 us
    psum x4, waiting for transfers between devices, run_slot(): lax.psum(input_back.astype(jnp.bfloat16), 'tensor').astype(jnp.float32)  108 us
    psum x4, waiting for transfers between devices, run_slot(): lax.psum(up_back.astype(jnp.bfloat16), 'tensor').astype(jnp.float32)  99.8 us
    psum x1, blocking collectives, per_device(): summed = lax.psum(totals, 'dp')  39.6 us
    while x496, local copies, waits for them, and re-layouts  30.9 us
    dot_general x4, matrix products, run_slot(): hidden_pre = jnp.dot(first_low, w_up, preferred_element_type=f32) + b_up  21.6 us
  transfers between devices with their start and end apart: 17, of which 17 were waited for; matrix products, arithmetic and copies ran while one was open for 7% of the time, Pallas kernels for 0%

commit v1 on v0

--- a/solution.py
+++ b/solution.py
@@ -79,19 +79,14 @@
     probs_low = attn_probs.astype(bf16)
     context = jnp.einsum("hqk,khd->qhd", probs_low, value_heads, preferred_element_type=f32)
     context = context.reshape(SEQ, -1).astype(bf16)
-    attn_out = lax.psum(jnp.dot(context, w_out, preferred_element_type=f32), "tensor") + b_out
+    attn_out = jnp.dot(context, w_out, preferred_element_type=f32) + b_out
     resid_one = tok_rows.astype(f32) + attn_out
     first_out, first_normed, first_inv = normalize(resid_one, attn_gain, attn_shift)
     first_low = first_out.astype(bf16)
     hidden_pre = jnp.dot(first_low, w_up, preferred_element_type=f32) + b_up
     hidden_act, gelu_pull = jax.vjp(gelu_exact, hidden_pre)
     hidden_low = hidden_act.astype(bf16)
-    ffn_out = (
-        lax.psum(
-            jnp.dot(hidden_low, w_down, preferred_element_type=f32).astype(jnp.bfloat16), "tensor"
-        ).astype(jnp.float32)
-        + b_down
-    )
+    ffn_out = jnp.dot(hidden_low, w_down, preferred_element_type=f32) + b_down
     resid_two = first_out + ffn_out
     layer_rows, second_normed, second_inv = normalize(resid_two, ffn_gain, ffn_shift)
     grad_ffn_gain = jnp.sum(grad_rows * second_normed, 0)
@@ -105,9 +100,7 @@
     grad_b_up = column_sum(grad_pre_low)
     grad_w_up = jnp.einsum("rd,rf->df", first_low, grad_pre_low, preferred_element_type=f32)
     up_back = jnp.einsum("rf,df->rd", grad_pre_low, w_up, preferred_element_type=f32)
-    grad_first = grad_resid_two + lax.psum(up_back.astype(jnp.bfloat16), "tensor").astype(
-        jnp.float32
-    )
+    grad_first = grad_resid_two + up_back
     grad_attn_gain = jnp.sum(grad_first * first_normed, 0)
     grad_attn_shift = jnp.sum(grad_first, 0)
     grad_resid_one = norm_back(grad_first * attn_gain, first_normed, first_inv)
@@ -142,9 +135,7 @@
         + jnp.einsum("rc,dc->rd", grad_key, w_key, preferred_element_type=f32)
         + jnp.einsum("rc,dc->rd", grad_value, w_value, preferred_element_type=f32)
     )
-    grad_tok = grad_resid_one + lax.psum(input_back.astype(jnp.bfloat16), "tensor").astype(
-        jnp.float32
-    )
+    grad_tok = grad_resid_one + input_back
     layer_low = (layer_rows * live_factor).astype(bf16)
     grad_low = grad_tok.astype(bf16)
     grads = (
@@ -167,87 +158,34 @@
     return (layer_low, grad_low, grads)
 
 
-def place_slot(carry, slot_index, layer_low, grad_low, grads):
-    out_buffer, grad_buffer, totals = carry
-    row_start = slot_index * SEQ
-    out_buffer = lax.dynamic_update_slice_in_dim(out_buffer, layer_low, row_start, 0)
-    grad_buffer = lax.dynamic_update_slice_in_dim(grad_buffer, grad_low, row_start, 0)
-    totals = jax.tree.map(jnp.add, totals, grads)
-    return (out_buffer, grad_buffer, totals)
-
-
-def per_device(
-    tokens,
-    cotangent,
-    key_lengths,
-    slot_counts,
-    w_query,
-    b_query,
-    w_key,
-    w_value,
-    b_value,
-    w_out,
-    b_out,
-    attn_gain,
-    attn_shift,
-    w_up,
-    b_up,
-    w_down,
-    b_down,
-    ffn_gain,
-    ffn_shift,
-):
-    params = (
-        w_query,
-        b_query,
-        w_key,
-        w_value,
-        b_value,
-        w_out,
-        b_out,
-        attn_gain,
-        attn_shift,
-        w_up,
-        b_up,
-        w_down,
-        b_down,
-        ffn_gain,
-        ffn_shift,
-    )
-    slot_total = key_lengths.shape[0]
-    live_count = slot_counts[0]
-    zero_grads = tuple((jnp.zeros(weight.shape, jnp.float32) for weight in params))
-    state = (jnp.zeros_like(tokens), jnp.zeros_like(tokens), zero_grads)
-
-    def masked_step(slot_index, carry):
-        live_factor = (slot_index < live_count).astype(jnp.float32)
-        layer_low, grad_low, grads = run_slot(
-            slot_index, live_factor, tokens, cotangent, key_lengths, params
-        )
-        return place_slot(carry, slot_index, layer_low, grad_low, grads)
-
-    state = lax.fori_loop(0, slot_total, masked_step, state)
-    layer_out, grad_tokens, totals = state
-    summed = lax.psum(totals, "dp")
-    return (
-        layer_out,
-        grad_tokens,
-        summed[0],
-        summed[1],
-        summed[2],
-        summed[3],
-        summed[4],
-        summed[5],
-        summed[6],
-        summed[7],
-        summed[8],
-        summed[9],
-        summed[10],
-        summed[11],
-        summed[12],
-        summed[13],
-        summed[14],
-    )
+SPLIT = {0: 1, 1: 0, 2: 1, 3: 1, 4: 0, 5: 0, 9: 1, 10: 0, 11: 0}
+
+
+def per_device(tokens, cotangent, key_lengths, slot_counts, *params):
+    f32 = jnp.float32
+    bf16 = jnp.bfloat16
+    slot_index = lax.axis_index("tensor")
+    full = tuple(
+        lax.all_gather(p, "tensor", axis=SPLIT[i], tiled=True) if i in SPLIT else p
+        for i, p in enumerate(params)
+    )
+    live_factor = (slot_index < slot_counts[0]).astype(f32)
+    layer_low, grad_low, grads = run_slot(
+        slot_index, live_factor, tokens, cotangent, key_lengths, full
+    )
+    layer_out = lax.all_gather(layer_low, "tensor", axis=0, tiled=True)
+    grad_tokens = lax.all_gather(grad_low, "tensor", axis=0, tiled=True)
+    outs = []
+    for i, g in enumerate(grads):
+        if g.ndim == 2:
+            g = lax.psum_scatter(g.astype(bf16), "tensor", scatter_dimension=SPLIT[i], tiled=True)
+            outs.append(lax.psum(g, "dp").astype(f32))
+        elif i in SPLIT:
+            g = lax.psum_scatter(g, "tensor", scatter_dimension=0, tiled=True)
+            outs.append(lax.psum(g, "dp"))
+        else:
+            outs.append(lax.psum(g, ("dp", "tensor")))
+    return (layer_out, grad_tokens, *outs)
 
 
 def solution(mesh):

time: 1070 us -> 639 us (0.60)
  waiting for transfers between devices: 711 us -> 370 us
  other arithmetic: 80.9 us -> 25 us
  matrix products: 165 us -> 112 us
  blocking collectives: 39.6 us -> 84 us
  local copies, waits for them, and re-layouts: 49 us -> 20.4 us
    psum x17 -> x1, waiting for transfers between devices: 710 us -> 132 us  [per_device(): outs.append(lax.psum(g, 'dp').astype(f32))]
    reduce_scatter x0 -> x6, waiting for transfers between devices: none -> 144 us  [per_device(): lax.psum_scatter(g.astype(bf16), 'tensor', scatter_dimension=SPLIT[i], ti...]
    all_gather x0 -> x8, waiting for transfers between devices: none -> 88.9 us  [the longest x6 88.9 us: per_device(): lax.all_gather(p, 'tensor', axis=SPLIT[i], tiled=True)]
    reduce_sum x12 -> x0, other arithmetic: 33.4 us -> none  [the longest x8 17.1 us: normalize(): center = hidden - jnp.mean(hidden, -1, keepdims=True)]
    while x496 -> x0, local copies, waits for them, and re-layouts: 30.9 us -> none
    psum x1 -> x2, blocking collectives: 39.6 us -> 60 us  [the longest x1 37.8 us: per_device(): outs.append(lax.psum(g, ('dp', 'tensor')))]
    unnamed x0 -> x2, blocking collectives: none -> 18.6 us
    dynamic_update_slice x8 -> x0, other arithmetic: 13.7 us -> none  [the longest x4 8.67 us: place_slot(): lax.dynamic_update_slice_in_dim(grad_buffer, grad_low, row_start, 0)]
  transfers between devices with their start and end apart: 17 -> 15, of which waited for: 17 -> 11; matrix products, arithmetic and copies ran while one was open for 7% -> 16% of each run, Pallas kernels for 0% -> 0%
where the time goes in v1:
time: 639 us; the launch traced here: 630 us
  waiting for transfers between devices  370 us (58%)
  matrix products  112 us (18%)
  blocking collectives  84 us (13%)
  other arithmetic  25 us (4%)
  local copies, waits for them, and re-layouts  20.4 us (3%)
  between operations  17.6 us (3%)
    reduce_scatter x6, waiting for transfers between devices, per_device(): lax.psum_scatter(g.astype(bf16), 'tensor', scatter_dimension=SPLIT[i], ti...  144 us
    psum x1, waiting for transfers between devices, per_device(): outs.append(lax.psum(g, 'dp').astype(f32))  132 us
    all_gather x6, waiting for transfers between devices, per_device(): lax.all_gather(p, 'tensor', axis=SPLIT[i], tiled=True)  88.9 us
    psum x1, blocking collectives, per_device(): outs.append(lax.psum(g, ('dp', 'tensor')))  37.8 us
    psum x1, blocking collectives, per_device(): outs.append(lax.psum(g, 'dp'))  22.2 us
    dot_general x1, matrix products, run_slot(): hidden_pre = jnp.dot(first_low, w_up, preferred_element_type=f32) + b_up  19.7 us
    unnamed x2, blocking collectives  18.6 us
    unnamed x83, local copies, waits for them, and re-layouts  17.4 us
  transfers between devices with their start and end apart: 15, of which 11 were waited for; matrix products, arithmetic and copies ran while one was open for 16% of the time, Pallas kernels for 0%

profile of v1, /device:TPU:0, one launch (start us, length us, event | category | flops | bytes accessed | tf_op | source)
XLA Modules:
  0.0 629.7 jit_solution(8172602933978015342)
XLA Ops:
  15.0 8.4 %all-reduce.9 = (bf16[768]{0:T(1024)(128)(2,1)S(1)}, bf16[768]{0:T(1024)(128)(2,1)S(1)}) all-reduce(bf16[768]{0:T(1024)(128)(2,1)S(1)} %dynamic-update-slice, bf16[768]{0:T(1024)(128)(2,1)S(1)} %dynamic-update-slice.1), channel_id=1, replica_groups=mesh['dp'=8,'tensor'=4] {'tensor'}, use_global_device_ids=true, to_apply=%add | all-reduce | flops 1536 | bytes 6144
  23.5 5.4 all-gather
  32.6 16.4 %all-gather.14.cloned.1.call-done = bf16[768,768]{0,1:T(8,128)(2,1)} async-done(((bf16[768,192]{0,1:T(8,128)(2,1)}), bf16[768,768]{0,1:T(8,128)(2,1)}) %all-gather.14.cloned.1.call-update) | async-done | bytes 1179664 | tf_op jit(solution)/shard_map/all_gather | solution.py:169
  61.0 7.0 %all-gather.10.cloned.1.call-done = bf16[768,768]{0,1:T(8,128)(2,1)} async-done(((bf16[768,192]{0,1:T(8,128)(2,1)}), bf16[768,768]{0,1:T(8,128)(2,1)}) %all-gather.10.cloned.1.call-update) | async-done | bytes 1179664 | tf_op jit(solution)/shard_map/all_gather | solution.py:169
  70.7 7.1 %fusion.18 = bf16[12,64,512]{2,1,0:T(8,128)(2,1)S(1)} fusion(bf16[512,12,64]{0,2,1:T(8,128)(2,1)S(1)} %bitcast.62, f32[12,512,512]{1,2,0:T(8,128)} %copy-done, f32[12,512]{1,0:T(8,128)S(1)} %fusion, f32[12,512]{1,0:T(8,128)S(1)} %get-tuple-element.54), kind=kOutput, calls=%fused_computation.66 | convolution fusion | flops 412483584 | bytes 14204928 | tf_op jit(solution)/shard_map/hqk,khd->qhd/dot_general | solution.py:80
  77.8 9.2 %all-gather.16.cloned.1.call-done = bf16[768,768]{1,0:T(8,128)(2,1)} async-done(((bf16[192,768]{1,0:T(8,128)(2,1)}), bf16[768,768]{1,0:T(8,128)(2,1)}) %all-gather.16.cloned.1.call-update) | async-done | bytes 1179664 | tf_op jit(solution)/shard_map/all_gather | solution.py:169
  89.7 36.1 %all-gather.18.cloned.1.call-done = bf16[768,3072]{1,0:T(8,128)(2,1)} async-done(((bf16[768,768]{1,0:T(8,128)(2,1)}), bf16[768,3072]{1,0:T(8,128)(2,1)}) %all-gather.18.cloned.1.call-update) | async-done | bytes 4718608 | tf_op jit(solution)/shard_map/all_gather | solution.py:169
  125.8 19.7 %multiply_convert_fusion.1 = (bf16[512,3072]{1,0:T(8,128)(2,1)}, f32[512,3072]{1,0:T(8,128)}, f32[512,3072]{1,0:T(8,128)}) fusion(f32[3072]{0:T(1024)S(1)} %bitcast.72, bf16[768,3072]{1,0:T(8,128)(2,1)} %all-gather.18.cloned.1.call-done, f32[512,768]{1,0:T(8,128)S(1)} %get-tuple-element.57, f32[768]{0:T(1024)S(1)} %convert_element_type.187, ...), kind=kOutput, calls=%fused_computation.14 | convolution fusion | flops 2521694208 | bytes 22042624 | tf_op jit(solution)/shard_map/dot_general | solution.py:86
  145.5 19.1 %all-gather.20.cloned.1.call-done = bf16[3072,768]{1,0:T(8,128)(2,1)} async-done(((bf16[768,768]{1,0:T(8,128)(2,1)}), bf16[3072,768]{1,0:T(8,128)(2,1)}) %all-gather.20.cloned.1.call-update) | async-done | bytes 4718608 | tf_op jit(solution)/shard_map/all_gather | solution.py:169
  164.7 6.2 fusion.46
  173.7 9.5 %convert_reduce_fusion = (f32[3072]{0:T(1024)S(1)}, bf16[512,3072]{1,0:T(8,128)(2,1)}) fusion(f32[512,3072]{1,0:T(8,128)} %get-tuple-element.50, bf16[3072,768]{1,0:T(8,128)(2,1)S(1)} %copy-done.29, f32[512,768]{1,0:T(8,128)S(1)} %get-tuple-element.46, f32[512,3072]{1,0:T(8,128)} %get-tuple-element.58, f32[3072]{0:T(1024)S(1)} %bitcast.73), kind=kOutput, calls=%fused_computation.11 | convolution fusion | flops 2443047936 | bytes 22044672 | tf_op jit(solution)/shard_map/rd,fd->rf/dot_general | solution.py:98
  196.6 7.3 %convert_reduce_fusion.3 = (f32[12,64]{1,0:T(8,128)S(1)}, bf16[12,64,512]{2,1,0:T(8,128)(2,1)S(1)}) fusion(bf16[512,12,64]{0,2,1:T(8,128)(2,1)S(1)} %bitcast.58, f32[12,512,512]{1,2,0:T(8,128)} %copy-done, f32[12,512]{1,0:T(8,128)S(1)} %log_add_fusion), kind=kOutput, calls=%fused_computation.35 | convolution fusion | flops 410123520 | bytes 14183424 | tf_op jit(solution)/shard_map/hqk,qhd->khd/dot_general | solution.py:124
  207.8 6.4 %multiply_reduce_fusion = (f32[12,512]{1,0:T(8,128)S(1)}, f32[12,512,512]{1,2,0:T(8,128)S(1)}) fusion(f32[12,512,512]{1,2,0:T(8,128)} %copy-done, f32[12,512]{1,0:T(8,128)S(1)} %log_add_fusion, bf16[512,12,64]{0,2,1:T(8,128)(2,1)S(1)} %bitcast.59, bf16[512,12,64]{0,2,1:T(8,128)(2,1)} %bitcast.63), kind=kOutput, calls=%fused_computation.1 | convolution fusion | flops 412084224 | bytes 26787840 | tf_op jit(solution)/shard_map/qhd,khd->hqk/dot_general | solution.py:113
  214.2 6.9 %multiply_convert_fusion = bf16[12,512,512]{1,2,0:T(8,128)(2,1)S(1)} fusion(f32[12,512,512]{1,2,0:T(8,128)S(1)} %get-tuple-element.63, f32[12,512,512]{1,2,0:T(8,128)} %copy-done, f32[12,512]{1,0:T(8,128)S(1)} %get-tuple-element.62, f32[12,512]{1,0:T(8,128)S(1)} %log_add_fusion), kind=kLoop, calls=%fused_computation | loop fusion | flops 12582912 | bytes 31506432 | tf_op jit(solution)/shard_map/convert_element_type | solution.py:115
  237.1 6.5 %convolution_convert_fusion.1 = bf16[768,3072]{1,0:T(8,128)(2,1)} fusion(bf16[512,3072]{1,0:T(8,128)(2,1)} %get-tuple-element.69, f32[512,768]{1,0:T(8,128)S(1)} %copy-done.5, f32[768]{0:T(1024)S(1)} %convert_element_type.187, f32[768]{0:T(1024)S(1)} %convert_element_type.186, f32[512]{0:T(512)S(1)} %add_rsqrt_fusion.1, f32[512]{0:T(512)S(1)} %broadcast_multiply_fusion.5), kind=kOutput, calls=%fused_computation.30 | convolution fusion | flops 2420244480 | bytes 9447424 | tf_op jit(solution)/shard_map/rd,rf->df/dot_general | solution.py:101
  244.9 6.8 %convolution_convert_fusion = bf16[3072,768]{1,0:T(8,128)(2,1)} fusion(bf16[512,3072]{1,0:T(8,128)(2,1)} %get-tuple-element.49, f32[512,768]{1,0:T(8,128)S(1)} %copy-done.14), kind=kOutput, calls=%fused_computation.29 | convolution fusion | flops 2418671616 | bytes 9437184 | tf_op jit(solution)/shard_map/rf,rd->fd/dot_general | solution.py:97
  258.8 15.4 %reduce-scatter.7.cloned.1.call-done = bf16[768,192]{0,1:T(8,128)(2,1)} async-done(((bf16[768,768]{0,1:T(8,128)(2,1)}), bf16[768,192]{0,1:T(8,128)(2,1)}) %reduce-scatter.7.cloned.1.call-update) | async-done | bytes 294928 | tf_op jit(solution)/shard_map/reduce_scatter | solution.py:181
  274.2 28.1 %reduce-scatter.9.cloned.1.call-done = bf16[768,192]{0,1:T(8,128)(2,1)} async-done(((bf16[768,768]{0,1:T(8,128)(2,1)}), bf16[768,192]{0,1:T(8,128)(2,1)}) %reduce-scatter.9.cloned.1.call-update) | async-done | bytes 294928 | tf_op jit(solution)/shard_map/reduce_scatter | solution.py:181
  302.3 50.4 %reduce-scatter.15.cloned.1.call-done = bf16[768,768]{1,0:T(8,128)(2,1)} async-done(((bf16[768,3072]{1,0:T(8,128)(2,1)}), bf16[768,768]{1,0:T(8,128)(2,1)}) %reduce-scatter.15.cloned.1.call-update) | async-done | bytes 1179664 | tf_op jit(solution)/shard_map/reduce_scatter | solution.py:181
  352.7 50.4 %reduce-scatter.17.cloned.1.call-done = bf16[768,768]{1,0:T(8,128)(2,1)} async-done(((bf16[3072,768]{1,0:T(8,128)(2,1)}), bf16[768,768]{1,0:T(8,128)(2,1)}) %reduce-scatter.17.cloned.1.call-update) | async-done | bytes 1179664 | tf_op jit(solution)/shard_map/reduce_scatter | solution.py:181
  404.5 10.3 %all-reduce.7 = (f32[768]{0:T(1024)S(1)}, f32[768]{0:T(1024)S(1)}, f32[3072]{0:T(1024)S(1)}) all-reduce(f32[768]{0:T(1024)S(1)} %reduce_sum.186, f32[768]{0:T(1024)S(1)} %reduce_sum.188, f32[3072]{0:T(1024)S(1)} %get-tuple-element.68), channel_id=3, replica_groups=mesh['dp'=8,'tensor'=4] {'tensor'}, use_global_device_ids=true, to_apply=%region_14.15.clone | all-reduce | flops 4608 | bytes 36864
  415.0 22.2 %all-reduce.6 = (f32[192]{0:T(256)}, f32[192]{0:T(256)}, f32[768]{0:T(1024)}) all-reduce(f32[192]{0:T(256)S(1)} %dynamic-slice.3, f32[192]{0:T(256)S(1)} %dynamic-slice.5, f32[768]{0:T(1024)S(1)} %dynamic-slice.7), channel_id=1, replica_groups=mesh['dp'=8,'tensor'=4] {'dp'}, use_global_device_ids=true, to_apply=%region_15.16 | all-reduce | flops 1152 | bytes 9216 | tf_op jit(solution)/shard_map/psum | solution.py:185
  437.3 37.8 %all-reduce.5 = (f32[768]{0:T(1024)}, f32[768]{0:T(1024)}, f32[768]{0:T(1024)}, f32[768]{0:T(1024)}, f32[768]{0:T(1024)}, /*index=5*/f32[768]{0:T(1024)}) all-reduce(f32[768]{0:T(1024)S(1)} %get-tuple-element.47, f32[768]{0:T(1024)S(1)} %get-tuple-element.20, ...), channel_id=1, replica_groups=mesh['dp'=8,'tensor'=4] {'dp','tensor'}, use_global_device_ids=true, to_apply=%region_26.27 | all-reduce | flops 4608 | bytes 36864 | tf_op jit(solution)/shard_map/psum | solution.py:187
  475.0 132.4 %all-reduce.12.cloned.1.call-done = (bf16[768,192]{0,1:T(8,128)(2,1)}, bf16[768,192]{0,1:T(8,128)(2,1)}, bf16[768,192]{0,1:T(8,128)(2,1)}, bf16[192,768]{1,0:T(8...) async-done(((bf16[768,192]{0,1:T(8,128)(2,1)}, bf16[768,192]{0,1:T(8,128)(2,1)}, bf16[768,192]{0,1:T(8,128)(2,1)}, bf16[192,768]{1,0:T(8,128)(2,1)}, ...) | async-done | bytes 3538960 | tf_op jit(solution)/shard_map/psum | solution.py:182
  (172 shorter events, 87.3 us)
Async XLA Ops:
  7.2 16.1 %copy-start.28 = (bf16[768]{0:T(1024)(128)(2,1)S(1)}, bf16[768]{0:T(1024)(128)(2,1)}, u32[]{:S(2)}) copy-start(bf16[768]{0:T(1024)(128)(2,1)} %param.33) | copy-start | bytes 4612
  7.2 16.1 %copy-start.21 = (bf16[768]{0:T(1024)(128)(2,1)S(1)}, bf16[768]{0:T(1024)(128)(2,1)}, u32[]{:S(2)}) copy-start(bf16[768]{0:T(1024)(128)(2,1)} %param.30) | copy-start | bytes 4612
  7.3 16.1 %copy-start.22 = (bf16[768]{0:T(1024)(128)(2,1)S(1)}, bf16[768]{0:T(1024)(128)(2,1)}, u32[]{:S(2)}) copy-start(bf16[768]{0:T(1024)(128)(2,1)} %param.31) | copy-start | bytes 4612
  7.3 16.1 %copy-start.23 = (bf16[768]{0:T(1024)(128)(2,1)S(1)}, bf16[768]{0:T(1024)(128)(2,1)}, u32[]{:S(2)}) copy-start(bf16[768]{0:T(1024)(128)(2,1)} %param.36) | copy-start | bytes 4612
  7.3 16.2 %copy-start.24 = (bf16[768]{0:T(1024)(128)(2,1)S(1)}, bf16[768]{0:T(1024)(128)(2,1)}, u32[]{:S(2)}) copy-start(bf16[768]{0:T(1024)(128)(2,1)} %param.29) | copy-start | bytes 4612
  7.3 16.2 %copy-start.25 = (bf16[768]{0:T(1024)(128)(2,1)S(1)}, bf16[768]{0:T(1024)(128)(2,1)}, u32[]{:S(2)}) copy-start(bf16[768]{0:T(1024)(128)(2,1)} %param.35) | copy-start | bytes 4612
  7.3 16.2 %copy-start.26 = (bf16[768]{0:T(1024)(128)(2,1)S(1)}, bf16[768]{0:T(1024)(128)(2,1)}, u32[]{:S(2)}) copy-start(bf16[768]{0:T(1024)(128)(2,1)} %param.37) | copy-start | bytes 4612
  7.3 22.7 %all-gather.12.cloned.1.call-start = ((), (), s32[]{:S(2)}) async-start(), calls=%async_computation.7 | async-start | bytes 1474560 | tf_op jit(solution)/shard_map/all_gather | solution.py:169
  8.0 41.0 %all-gather.14.cloned.1.call-start = ((), (), s32[]{:S(2)}) async-start(), calls=%async_computation.8 | async-start | bytes 1474560 | tf_op jit(solution)/shard_map/all_gather | solution.py:169
  8.8 59.2 %all-gather.10.cloned.1.call-start = ((), (), s32[]{:S(2)}) async-start(), calls=%async_computation.6 | async-start | bytes 1474560 | tf_op jit(solution)/shard_map/all_gather | solution.py:169
  9.5 77.4 %all-gather.16.cloned.1.call-start = ((), (), s32[]{:S(2)}) async-start(), calls=%async_computation.9 | async-start | bytes 1474560 | tf_op jit(solution)/shard_map/all_gather | solution.py:169
  10.1 115.7 %all-gather.18.cloned.1.call-start = ((), (), s32[]{:S(2)}) async-start(), calls=%async_computation.10 | async-start | bytes 5898240 | tf_op jit(solution)/shard_map/all_gather | solution.py:169
  10.7 154.0 %all-gather.20.cloned.1.call-start = ((), (), s32[]{:S(2)}) async-start(), calls=%async_computation.11 | async-start | bytes 5898240 | tf_op jit(solution)/shard_map/all_gather | solution.py:169
  11.3 247.5 %reduce-scatter.13.cloned.1.call-start = ((), (), s32[]{:S(2)}) async-start(), calls=%async_computation.17 | async-start | bytes 1474560 | tf_op jit(solution)/shard_map/reduce_scatter | solution.py:181
  32.6 22.1 %copy-start.2 = (bf16[512,768]{0,1:T(8,128)(2,1)}, bf16[512,768]{0,1:T(8,128)(2,1)S(1)}, u32[]{:S(2)}) copy-start(bf16[512,768]{0,1:T(8,128)(2,1)S(1)} %copy.57) | copy-start | bytes 2359300
  89.4 93.8 %copy-start.4 = (f32[512,768]{1,0:T(8,128)}, f32[512,768]{1,0:T(8,128)S(1)}, u32[]{:S(2)}) copy-start(f32[512,768]{1,0:T(8,128)S(1)} %get-tuple-element.57) | copy-start | bytes 4718596
  192.0 66.8 %reduce-scatter.11.cloned.1.call-start = ((), (), s32[]{:S(2)}) async-start(), calls=%async_computation.16 | async-start | bytes 1474560 | tf_op jit(solution)/shard_map/reduce_scatter | solution.py:181
  207.8 66.5 %reduce-scatter.7.cloned.1.call-start = ((), (), s32[]{:S(2)}) async-start(), calls=%async_computation.14 | async-start | bytes 1474560 | tf_op jit(solution)/shard_map/reduce_scatter | solution.py:181
  227.8 74.5 %reduce-scatter.9.cloned.1.call-start = ((), (), s32[]{:S(2)}) async-start(), calls=%async_computation.15 | async-start | bytes 1474560 | tf_op jit(solution)/shard_map/reduce_scatter | solution.py:181
  237.0 115.7 %reduce-scatter.15.cloned.1.call-start = ((), (), s32[]{:S(2)}) async-start(), calls=%async_computation.18 | async-start | bytes 5898240 | tf_op jit(solution)/shard_map/reduce_scatter | solution.py:181
  243.6 159.5 %reduce-scatter.17.cloned.1.call-start = ((), (), s32[]{:S(2)}) async-start(), calls=%async_computation.19 | async-start | bytes 5898240 | tf_op jit(solution)/shard_map/reduce_scatter | solution.py:181
  251.7 223.3 %all-gather.22.cloned.1.call-start = ((), (), s32[]{:S(2)}) async-start(), calls=%async_computation.12 | async-start | bytes 3932160 | tf_op jit(solution)/shard_map/all_gather | solution.py:176
  252.5 222.6 %all-gather.24.cloned.1.call-start = ((), (), s32[]{:S(2)}) async-start(), calls=%async_computation.13 | async-start | bytes 3932160 | tf_op jit(solution)/shard_map/all_gather | solution.py:177
  258.7 348.7 %all-reduce.12.cloned.1.call-start = ((), (), s32[]{:S(2)}) async-start(), calls=%async_computation.20 | async-start | bytes 7077888 | tf_op jit(solution)/shard_map/psum | solution.py:182
  (27 other events, 120.5 us)
Sparse Core Ops, SparseCore 0:
  9.7 20.2 all-gather.11
  31.5 17.4 all-gather.13
  50.6 17.4 all-gather.9
  69.5 17.4 all-gather.15
  88.4 37.3 all-gather.17
  127.2 37.4 all-gather.19
  192.2 25.6 reduce-scatter.12
  220.4 25.6 reduce-scatter.10
  248.6 25.6 reduce-scatter.6
  276.7 25.6 reduce-scatter.8
  304.9 47.7 reduce-scatter.14
  355.1 47.9 reduce-scatter.16
  404.6 28.5 all-gather.21
  435.2 28.7 all-gather.23
  468.2 139.2 all-reduce.11

commit v2 on v1

v2 whole, which is shorter than its diff:
```python
import functools

import jax
import jax.numpy as jnp
from jax import lax
from jax.experimental import pallas as pl
from jax.experimental.pallas import tpu as pltpu
from jax.sharding import PartitionSpec as P

D = 768
HD = 64
SEQ = 512
MESH = pl.DeviceIdType.MESH
F32 = jnp.float32
BF16 = jnp.bfloat16
FF_PIECES = 6
PIECES = 10
LAG = {2: 1, 3: 3, 4: 4}


def flip(value, bit):
    return value + bit - 2 * bit * lax.rem(value // bit, 2)


def dot_nn(a, b):
    return lax.dot_general(a, b, (((1,), (0,)), ((), ())), preferred_element_type=F32)


def dot_nt(a, b):
    return lax.dot_general(a, b, (((1,), (1,)), ((), ())), preferred_element_type=F32)


def dot_tn(a, b):
    return lax.dot_general(a, b, (((0,), (0,)), ((), ())), preferred_element_type=F32)


def row_mean(value):
    return jnp.sum(value, -1, keepdims=True) * (1.0 / D)


def col_sum(value):
    return jnp.sum(value, 0, keepdims=True)


def norm_back(grad, normed, inv_std):
    return inv_std * (grad - row_mean(grad) - normed * row_mean(grad * normed))


def block(index, size):
    return pl.ds(pl.multiple_of(index * size, size), size)


def layer_kernel(dp_bits, tok_hbm, cot_hbm, len_ref, cnt_ref, qkv_own, out_own, up_own, down_own,
                 rows_ref, layer_out, grad_out, off_ref, oat_ref, vec_out,
                 wqkv, wo, wup, wdn, bias, tok, cot, qkv, ctx, lse, n1, r1, flow, hid, gd, gr2,
                 glow, acc, gctx, st, stage_rows, gff, r0, r1f, r2, r3, rx, rxa, vec_acc, vec_in,
                 ws, wr, gs, gr, vs, vr, os, orr, bs, br, ls, free_sem):
    t = lax.axis_index("tensor")
    d = lax.axis_index("dp")
    c = lax.rem(t, 2)
    x = t // 2
    b0 = lax.rem(d, 2)
    b1 = lax.rem(d // 2, 2)
    other = flip(t, 2)
    core = {"tensor": flip(t, 1)}
    across = {"tensor": other}
    dps = [{"dp": flip(d, 1 << k)} for k in range(dp_bits)]
    beside = dps[0]
    partners = (core, across, *dps)

    def send(src, dst, send_sem, recv_sem, device):
        return pltpu.make_async_remote_copy(
            src_ref=src, dst_ref=dst, send_sem=send_sem, recv_sem=recv_sem,
            device_id=device, device_id_type=MESH,
        )

    def slot_of(order):
        oc = lax.rem(order, 2)
        ox = order // 2
        return (x + ox - 2 * x * ox) * 2 + c + oc - 2 * c * oc

    loads = [
        pltpu.make_async_copy(tok_hbm.at[block(t, SEQ)], tok, ls.at[0]),
        pltpu.make_async_copy(qkv_own, wqkv.at[t], ls.at[1]),
        pltpu.make_async_copy(out_own, wo.at[t], ls.at[2]),
        pltpu.make_async_copy(up_own, wup.at[t], ls.at[3]),
        pltpu.make_async_copy(down_own, wdn.at[t], ls.at[4]),
        pltpu.make_async_copy(cot_hbm.at[block(t, SEQ)], cot, ls.at[5]),
    ]
    for load in loads:
        load.start()
    bias[t] = rows_ref[8:16]
    barrier = pltpu.get_barrier_semaphore()
    for device in partners:
        pl.semaphore_signal(barrier, inc=1, device_id=device, device_id_type=MESH)
    pl.semaphore_wait(barrier, len(partners))

    mine8 = rows_ref.at[pl.ds(8, 8)]
    bias_hop = send(mine8, bias.at[t], bs.at[0], br.at[0], across)
    bias_chip = send(mine8, bias.at[t], bs.at[1], br.at[1], core)
    bias_mate = send(bias.at[other], bias.at[other], bs.at[2], br.at[2], core)
    bias_hop.start()
    bias_chip.start()

    half_up = up_own.shape[0] // 2
    half_down = down_own.shape[0] // 2
    chunks = [
        (qkv_own, wqkv, 0, qkv_own.shape[0]), (out_own, wo, 0, out_own.shape[0]),
        (up_own, wup, 0, half_up), (up_own, wup, half_up, half_up),
        (down_own, wdn, 0, half_down), (down_own, wdn, half_down, half_down),
    ]

    def span(base, rows, which):
        return pl.ds(pl.multiple_of(base + which * (rows // 2), 16), rows // 2)

    hops, chips, relays, mates, lasts = [], [], [], [], []
    for i, (own, full, base, rows) in enumerate(chunks):
        hops.append(send(own.at[span(base, rows, b0)], full.at[t, span(base, rows, b0)],
                         ws.at[i, 1], wr.at[i, 1], across))
        chips.append(send(own.at[pl.ds(base, rows)], full.at[t, pl.ds(base, rows)],
                          ws.at[i, 0], wr.at[i, 0], core))
        here = full.at[other, span(base, rows, b0)]
        there = full.at[other, span(base, rows, 1 - b0)]
        relays.append(send(here, here, ws.at[i, 2], wr.at[i, 2], beside))
        mates.append(send(here, here, ws.at[i, 3], wr.at[i, 3], core))
        lasts.append(send(there, there, ws.at[i, 4], wr.at[i, 4], core))
        hops[i].start()
        chips[i].start()

    def from_across(i):
        hops[i].wait()
        relays[i].start()
        mates[i].start()

    def from_beside(i):
        relays[i].wait()
        lasts[i].start()

    def from_core(i):
        chips[i].wait()

    def from_far(i):
        mates[i].wait()
        lasts[i].wait()

    live = jnp.where(t < cnt_ref[0], 1.0, 0.0).astype(F32)
    length = len_ref[t]
    key_mask = jnp.where(
        lax.broadcasted_iota(jnp.int32, (1, SEQ), 1) < length, 0.0, -1e30
    ).astype(F32)
    vec_acc[0] = jnp.zeros_like(vec_acc[0])
    vec = vec_acc.at[0]

    def add_vec(row, value):
        vec[pl.ds(row, 1)] = vec[pl.ds(row, 1)] + value

    loads[0].wait()
    loads[1].wait()

    def attend(order, carry):
        s = slot_of(order)

        @pl.when(order == 1)
        def _():
            from_across(0)
            bias_hop.wait()
            bias_mate.start()
            from_core(0)
            bias_chip.wait()

        @pl.when(order == 2)
        def _():
            from_across(1)
            from_beside(0)
            bias_mate.wait()

        @pl.when(order == 3)
        def _():
            from_beside(1)
            from_far(0)

        for j in range(3):
            h = 3 * s + j
            w_rows = wqkv[s, 192 * j:192 * (j + 1)]
            qkv[h] = (dot_nt(tok[...], w_rows) + bias[s, 1 + j:2 + j, 0:192]).astype(BF16)
            keys = qkv[h, :, 64:128]
            values = qkv[h, :, 128:192]

            def rows(rb, carry):
                at = block(rb, 128)
                scores = dot_nt(qkv[h, at, 0:64], keys) * 0.125 + key_mask
                top = jnp.max(scores, -1, keepdims=True)
                expd = jnp.exp(scores - top)
                total = jnp.sum(expd, -1, keepdims=True)
                probs = (expd * (1.0 / total)).astype(BF16)
                ctx[s, at, 64 * j:64 * (j + 1)] = dot_nn(probs, values).astype(BF16)
                lane = lax.broadcasted_iota(jnp.int32, (128, 128), 1)
                lse[s, at] = jnp.where(lane == j, top + jnp.log(total), lse[s, at])
                return carry

            lax.fori_loop(0, SEQ // 128, rows, 0)
        return carry

    lse[...] = jnp.zeros_like(lse)
    lax.fori_loop(0, 4, attend, 0)

    from_across(2)
    from_core(1)
    from_far(1)
    loads[2].wait()
    gain1 = rows_ref[1:2]
    shift1 = rows_ref[2:3]

    def project(rb, carry):
        at = block(rb, 128)
        total = tok[at].astype(F32) + rows_ref[0:1]
        for s in range(4):
            total = total + dot_nn(ctx[s, at], wo[s])
        center = total - row_mean(total)
        inv = lax.rsqrt(row_mean(center * center) + 1e-5)
        normed = center * inv
        out = normed * gain1 + shift1
        n1[at] = normed
        r1[at] = inv
        flow[at] = out.astype(BF16)
        acc[at] = out + rows_ref[3:4]
        return carry

    lax.fori_loop(0, 4, project, 0)

    from_across(3)
    loads[3].wait()

    def raise_up(order, carry):
        s = slot_of(order)

        @pl.when(order == 1)
        def _():
            from_beside(2)
            from_core(2)
            from_core(3)

        @pl.when(order == 2)
        def _():
            from_across(4)
            from_beside(3)

        @pl.when(order == 3)
        def _():
            from_far(2)
            from_far(3)

        def rows(rb, carry):
            at = block(rb, 128)
            pre = dot_nn(flow[at], wup[s]) + bias[s, 0:1]
            cdf = 0.5 + 0.5 * lax.erf(pre * 0.7071067811865476)
            pdf = jnp.exp(pre * pre * -0.5) * 0.3989422804014327
            hid[s, at] = (pre * cdf).astype(BF16)
            gd[s, at] = (cdf + pre * pdf).astype(BF16)
            return carry

        lax.fori_loop(0, 4, rows, 0)
        return carry

    lax.fori_loop(0, 4, raise_up, 0)
    from_across(5)
    from_beside(4)
    loads[4].wait()

    def bring_down(order, carry):
        s = slot_of(order)

        @pl.when(order == 1)
        def _():
            from_core(4)
            from_core(5)

        @pl.when(order == 2)
        def _():
            from_beside(5)

        @pl.when(order == 3)
        def _():
            from_far(4)
            from_far(5)

        def rows(rb, carry):
            at = block(rb, 256)
            acc[at] = acc[at] + dot_nn(hid[s, at], wdn[s])
            return carry

        lax.fori_loop(0, 2, rows, 0)
        return carry

    lax.fori_loop(0, 4, bring_down, 0)

    loads[5].wait()
    gain2 = rows_ref[4:5]
    shift2 = rows_ref[5:6]
    lay = stage_rows.at[0]
    gtok = stage_rows.at[1]

    def second(rb, carry):
        at = block(rb, 128)
        total = acc[at]
        center = total - row_mean(total)
        inv = lax.rsqrt(row_mean(center * center) + 1e-5)
        normed = center * inv
        lay[at] = (live * (normed * gain2 + shift2)).astype(BF16)
        grad = live * cot[at].astype(F32)
        add_vec(1, col_sum(grad * normed))
        add_vec(2, col_sum(grad))
        back = norm_back(grad * gain2, normed, inv)
        low = back.astype(BF16)
        gr2[at] = back
        glow[at] = low
        add_vec(0, col_sum(low.astype(F32)))
        acc[at] = jnp.zeros_like(total)
        return carry

    lax.fori_loop(0, 4, second, 0)

    def spread(i, src, dst):
        return (
            pltpu.make_async_copy(src, dst.at[t], ls.at[6 + i]),
            send(src, dst.at[t], os.at[i, 0], orr.at[i, 0], across),
            send(src, dst.at[t], os.at[i, 1], orr.at[i, 1], core),
            send(dst.at[other], dst.at[other], os.at[i, 2], orr.at[i, 2], core),
        )

    lay_copies = spread(0, lay, layer_out)
    for copy in lay_copies[:3]:
        copy.start()

    n_exchange = dp_bits - 2
    last = 4 + n_exchange + 2
    lag = dict(LAG)
    for s in range(5, last + 1):
        lag[s] = lag[s - 1] + (2 if s == last else 1)

    def att_rows(shard, quarter, count):
        return pl.ds(pl.multiple_of((shard * 4 + quarter) * 48, 48), count)

    def views(ff, p):
        out = off_ref if ff else oat_ref
        if ff:
            return dict(
                s0=gff.at[p, 1 - c], k0=gff.at[p, c], r0=r0.at[p],
                s1=gff.at[p, c, 1 - x], k1=gff.at[p, c, x], r1=r1f.at[p],
                s2=gff.at[p, c, x, 1 - b0], k2=gff.at[p, c, x, b0], r2=r2.at[p],
                s3=gff.at[p, c, x, b0, 1 - b1], k3=gff.at[p, c, x, b0, b1], r3=r3.at[p],
                rx=rx, o1=out.at[p, b0, b1], o0=out.at[p, b0],
            )
        g = wdn.at[p]
        r = wup.at[p]
        me = 2 * c + x
        return dict(
            s0=g.at[att_rows(2 * (1 - c), 0, 384)], k0=g.at[att_rows(2 * c, 0, 384)],
            r0=r.at[pl.ds(0, 384)],
            s1=g.at[att_rows(2 * c + 1 - x, 0, 192)], k1=g.at[att_rows(me, 0, 192)],
            r1=r.at[pl.ds(384, 192)],
            s2=g.at[att_rows(me, 2 * (1 - b0), 96)], k2=g.at[att_rows(me, 2 * b0, 96)],
            r2=r.at[pl.ds(576, 96)],
            s3=g.at[att_rows(me, 2 * b0 + 1 - b1, 48)], k3=g.at[att_rows(me, 2 * b0 + b1, 48)],
            r3=r.at[pl.ds(672, 48)],
            rx=rxa, o1=out.at[p, b0, b1], o0=out.at[p, b0],
        )

    def stage_copy(s, p, ff):
        v = views(ff, p)
        base = 0 if ff else FF_PIECES
        sems = (gs.at[s, base + p], gr.at[s, base + p])
        if s < 4:
            return send(v[f"s{s}"], v[f"r{s}"], *sems, (core, across, dps[0], dps[1])[s])
        if s < 4 + n_exchange:
            k = s - 4
            return send(v["k3"], v["rx"].at[p, k], *sems, dps[2 + k])
        if s == 4 + n_exchange:
            return send(v["o1"], v["o1"], *sems, dps[1])
        return send(v["o0"], v["o0"], *sems, dps[0])

    def combine(s, p, ff):
        v = views(ff, p)
        if s < 4:
            keep, got = v[f"k{s}"], v[f"r{s}"]
            keep[...] = keep[...] + got[...]
        elif s < 4 + n_exchange:
            k = s - 4
            total = v["k3"][...] + v["rx"].at[p, k][...]
            v["o1" if k == n_exchange - 1 else "k3"][...] = total

    def run_stage(s, p, ff):
        if s > 0:
            stage_copy(s - 1, p, ff).wait()
            combine(s - 1, p, ff)
        if s < last:
            stage_copy(s, p, ff).start()

    def down_grad(i, carry):
        def shard(s, carry):
            value = dot_tn(hid[s, :, block(i, 256)], glow[...]).astype(BF16)
            for q in range(4):
                gff[i, lax.rem(s, 2), s // 2, q // 2, q % 2] = value[64 * q:64 * (q + 1)]
            return carry

        lax.fori_loop(0, 4, shard, 0)
        run_stage(0, i, True)

        @pl.when(i > 0)
        def _():
            run_stage(1, i - 1, True)

        return carry

    lax.fori_loop(0, 3, down_grad, 0)

    def ffn_back(s, carry):
        @pl.when(s == 1)
        def _():
            run_stage(1, 2, True)
            lay_copies[1].wait()
            lay_copies[3].start()

        def rows(rb, carry):
            at = block(rb, 256)
            low = (dot_nt(glow[at], wdn[s]) * gd[s, at].astype(F32)).astype(BF16)
            gd[s, at] = low
            add_vec(8 + s, col_sum(low.astype(F32)))
            acc[at] = acc[at] + dot_nt(low, wup[s])
            return carry

        lax.fori_loop(0, 2, rows, 0)
        return carry

    lax.fori_loop(0, 4, ffn_back, 0)
    for device in partners:
        pl.semaphore_signal(free_sem, inc=1, device_id=device, device_id_type=MESH)

    def up_grad(i, carry):
        def shard(s, carry):
            value = dot_tn(flow[:, block(i, 256)], gd[s]).astype(BF16)
            for q in range(4):
                gff[3 + i, lax.rem(s, 2), s // 2, q // 2, q % 2] = value[64 * q:64 * (q + 1)]
            return carry

        lax.fori_loop(0, 4, shard, 0)
        run_stage(0, 3 + i, True)

        @pl.when(i > 0)
        def _():
            run_stage(1, 2 + i, True)

        return carry

    lax.fori_loop(0, 3, up_grad, 0)

    def first_back(rb, carry):
        at = block(rb, 128)
        grad = gr2[at] + acc[at]
        normed = n1[at]
        add_vec(4, col_sum(grad * normed))
        add_vec(5, col_sum(grad))
        back = norm_back(grad * gain1, normed, r1[at])
        low = back.astype(BF16)
        acc[at] = back
        glow[at] = low
        add_vec(3, col_sum(low.astype(F32)))
        return carry

    lax.fori_loop(0, 4, first_back, 0)
    run_stage(1, 5, True)

    pl.semaphore_wait(free_sem, len(partners))

    def out_back(s, carry):
        home = att_rows(2 * lax.rem(s, 2) + s // 2, 0, 192)
        wdn[0, home] = dot_tn(ctx[s], glow[...]).astype(BF16)
        back = dot_nt(glow[...], wo[s]).astype(BF16)
        for j in range(3):
            gctx[3 * s + j] = back[:, 64 * j:64 * (j + 1)]
        return carry

    lax.fori_loop(0, 4, out_back, 0)
    run_stage(0, 0, False)

    def tail_stages(n):
        for s in range(last, 1, -1):
            for ff in (True, False):
                p = (n - lag[s]) // 3
                low, high = (0, FF_PIECES) if ff else (FF_PIECES, PIECES)

                @pl.when((n >= lag[s]) & (lax.rem(n + 300 - lag[s], 3) == 0) & (p >= low) & (p < high))
                def _():
                    run_stage(s, p - low, ff)

    def head_back(n, carry):
        s = slot_of(lax.rem(n, 4))
        j = n // 4
        h = 3 * s + j
        keys = qkv[h, :, 64:128]
        values = qkv[h, :, 128:192]
        keys_t = keys.T
        st[...] = jnp.zeros_like(st)

        def rows(rb, carry):
            at = block(rb, 128)
            query = qkv[h, at, 0:64]
            gout = gctx[h, at]
            lane = lax.broadcasted_iota(jnp.int32, (128, 128), 1)
            norm = jnp.sum(jnp.where(lane == j, lse[s, at], 0.0), -1, keepdims=True)
            probs = jnp.exp(dot_nt(query, keys) * 0.125 + key_mask - norm)
            gprobs = dot_nt(gout, values)
            scored = probs * (gprobs - jnp.sum(gprobs * probs, -1, keepdims=True))
            scored = scored.astype(BF16)
            st[0:64, at] = dot_nt(keys_t, scored)
            st[64:128] = st[64:128] + dot_tn(query, scored)
            st[128:192] = st[128:192] + dot_tn(gout, probs.astype(BF16))
            return carry

        lax.fori_loop(0, SEQ // 128, rows, 0)
        row = lax.broadcasted_iota(jnp.int32, (192, 1), 0)
        packed = (st[...] * jnp.where(row < 128, 0.125, 1.0)).astype(BF16)
        home = att_rows(2 * lax.rem(s, 2) + s // 2, 0, 192)
        wdn[1 + j, home] = dot_nn(packed, tok[...]).astype(BF16)
        sums = dot_nt(jnp.ones((8, SEQ), BF16), packed)
        vec[pl.ds(12 + h, 1), 0:192] = sums[0:1]
        w_rows = wqkv[s, block(j, 192)]

        acc[...] = acc[...] + dot_tn(packed, w_rows)

        @pl.when(n == 0)
        def _():
            run_stage(1, 0, False)

        @pl.when(lax.rem(n, 4) == 3)
        def _():
            run_stage(0, 1 + j, False)

        @pl.when((n > 0) & (lax.rem(n, 4) == 0))
        def _():
            run_stage(1, j, False)

        tail_stages(n)
        return carry

    lax.fori_loop(0, 12, head_back, 0)
    gtok[...] = acc[...].astype(BF16)
    tok_copies = spread(1, gtok, grad_out)
    for copy in tok_copies[:3]:
        copy.start()

    def vec_copy(k):
        return send(vec_acc.at[k], vec_in.at[k], vs.at[k], vr.at[k], partners[k])

    vec_copy(0).start()
    run_stage(1, 3, False)
    end = max(3 * (PIECES - 1) + lag[last], 13 + 2 * len(partners))

    def drain(n, carry):
        tail_stages(n)
        for k in range(len(partners)):
            @pl.when(n == 14 + 2 * k)
            def _():
                vec_copy(k).wait()
                total = vec_acc[k] + vec_in[k]
                if k == len(partners) - 1:
                    vec_out[...] = total
                else:
                    vec_acc[k + 1] = total
                    vec_copy(k + 1).start()

        @pl.when(n == 30)
        def _():
            tok_copies[1].wait()
            tok_copies[3].start()

        return carry

    lax.fori_loop(12, end + 1, drain, 0)
    for copies in (lay_copies, tok_copies):
        copies[0].wait()
        copies[2].wait()
        copies[3].wait()


def run_layer(dp, tokens, cotangent, key_lengths, slot_counts, shards, rows):
    dp_bits = dp.bit_length() - 1
    n_exchange = dp_bits - 2
    stages = 4 + n_exchange + 2
    links = dp_bits + 2
    vmem = pl.BlockSpec(memory_space=pltpu.VMEM)
    smem = pl.BlockSpec(memory_space=pltpu.SMEM)
    hbm = pl.BlockSpec(memory_space=pltpu.HBM)
    dma = pltpu.SemaphoreType.DMA
    return pl.pallas_call(
        functools.partial(layer_kernel, dp_bits),
        out_shape=[
            jax.ShapeDtypeStruct((4, SEQ, D), BF16),
            jax.ShapeDtypeStruct((4, SEQ, D), BF16),
            jax.ShapeDtypeStruct((6, 2, 2, 64, D), BF16),
            jax.ShapeDtypeStruct((4, 2, 2, 48, D), BF16),
            jax.ShapeDtypeStruct((24, D), F32),
        ],
        in_specs=[hbm, hbm, smem, smem] + [hbm] * 4 + [vmem],
        out_specs=[hbm] * 2 + [vmem] * 3,
        scratch_shapes=[
            *[pltpu.VMEM((4, *s.shape), BF16) for s in shards],
            pltpu.VMEM((4, 8, D), F32),
            pltpu.VMEM((SEQ, D), BF16),
            pltpu.VMEM((SEQ, D), BF16),
            pltpu.VMEM((12, SEQ, 192), BF16),
            pltpu.VMEM((4, SEQ, 192), BF16),
            pltpu.VMEM((4, SEQ, 128), F32),
            pltpu.VMEM((SEQ, D), F32),
            pltpu.VMEM((SEQ, 1), F32),
            pltpu.VMEM((SEQ, D), BF16),
            pltpu.VMEM((4, SEQ, D), BF16),
            pltpu.VMEM((4, SEQ, D), BF16),
            pltpu.VMEM((SEQ, D), F32),
            pltpu.VMEM((SEQ, D), BF16),
            pltpu.VMEM((SEQ, D), F32),
            pltpu.VMEM((12, SEQ, 64), BF16),
            pltpu.VMEM((192, SEQ), F32),
            pltpu.VMEM((2, SEQ, D), BF16),
            pltpu.VMEM((6, 2, 2, 2, 2, 64, D), BF16),
            pltpu.VMEM((6, 2, 2, 2, 64, D), BF16),
            pltpu.VMEM((6, 2, 2, 64, D), BF16),
            pltpu.VMEM((6, 2, 64, D), BF16),
            pltpu.VMEM((6, 64, D), BF16),
            pltpu.VMEM((6, n_exchange, 64, D), BF16),
            pltpu.VMEM((4, n_exchange, 48, D), BF16),
            pltpu.VMEM((links, 24, D), F32),
            pltpu.VMEM((links, 24, D), F32),
            dma((6, 5)), dma((6, 5)),
            dma((stages, PIECES)), dma((stages, PIECES)),
            dma((links,)), dma((links,)),
            dma((2, 3)), dma((2, 3)),
            dma((3,)), dma((3,)),
            dma((8,)),
            pltpu.SemaphoreType.REGULAR,
        ],
        compiler_params=pltpu.CompilerParams(
            collective_id=0, has_side_effects=True, vmem_limit_bytes=67043328
        ),
    )(tokens, cotangent, key_lengths, slot_counts, *shards, rows)


def per_device(dp, tokens, cotangent, key_lengths, slot_counts, *params):
    (w_query, b_query, w_key, w_value, b_value, w_out, b_out, attn_gain, attn_shift,
     w_up, b_up, w_down, b_down, ffn_gain, ffn_shift) = params
    slot = lax.axis_index("tensor")
    heads = w_query.shape[1] // HD
    qkv = jnp.stack([w.reshape(D, heads, HD) for w in (w_query, w_key, w_value)], 1)
    qkv = qkv.transpose(2, 1, 3, 0).reshape(-1, D)
    q_bias = b_query.reshape(heads, HD)
    v_bias = b_value.reshape(heads, HD)
    qkv_bias = jnp.concatenate(
        (q_bias, jnp.zeros_like(q_bias), v_bias, jnp.zeros((heads, D - 3 * HD), BF16)), 1
    )
    rows = jnp.concatenate(
        [v[None] for v in (b_out, attn_gain, attn_shift, b_down, ffn_gain, ffn_shift)]
        + [jnp.zeros((2, D), BF16), b_up[None], qkv_bias, jnp.zeros((4, D), BF16)], 0
    ).astype(F32)
    layer, grad, off, oat, vec = run_layer(
        dp, tokens, cotangent, key_lengths, slot_counts, (qkv, w_out, w_up, w_down), rows
    )
    off = off.reshape(2, -1, D).astype(F32)
    oat = oat.reshape(4, -1, D)
    g_out = oat[0].astype(F32)
    g_qkv = oat[1:].reshape(heads, 3, HD, D)
    g_q, g_k, g_v = (g_qkv[:, i].reshape(-1, D).T.astype(F32) for i in range(3))
    b_qkv = lax.dynamic_slice_in_dim(vec[12:, :3 * HD], slot * heads, heads)
    gb_up = lax.dynamic_slice_in_dim(vec[8:12], slot, 1)[0]
    return (layer.reshape(-1, D), grad.reshape(-1, D),
            g_q, b_qkv[:, :HD].reshape(-1), g_k, g_v, b_qkv[:, 2 * HD:].reshape(-1), g_out,
            vec[3], vec[4], vec[5], off[1], gb_up, off[0], vec[0], vec[1], vec[2])


def solution(mesh):
    placed = (
        P("dp", None),
        P("dp", None),
        P("dp"),
        P("dp"),
        P(None, "tensor"),
        P("tensor"),
        P(None, "tensor"),
        P(None, "tensor"),
        P("tensor"),
        P("tensor", None),
        P(),
        P(),
        P(),
        P(None, "tensor"),
        P("tensor"),
        P("tensor", None),
        P(),
        P(),
        P(),
    )
    return jax.shard_map(
        functools.partial(per_device, mesh.shape["dp"]),
        mesh=mesh,
        in_specs=placed,
        out_specs=(
            P("dp", None),
            P("dp", None),
            P(None, "tensor"),
            P("tensor"),
            P(None, "tensor"),
            P(None, "tensor"),
            P("tensor"),
            P("tensor", None),
            P(),
            P(),
            P(),
            P(None, "tensor"),
            P("tensor"),
            P("tensor", None),
            P(),
            P(),
            P(),
        ),
        check_vma=False,
    )
```

time: 639 us -> 287 us (0.45); the launches traced: 630 us -> 286 us
  waiting for transfers between devices: 370 us -> 0 us
  Pallas kernels: 0 us -> 259 us
  matrix products: 112 us -> 0 us
  blocking collectives: 84 us -> 0 us
  other arithmetic: 25 us -> 5.66 us
  between operations: 17.6 us -> 1.35 us
    pallas_call x0 -> x1, Pallas kernels: none -> 259 us  [run_layer(): pl.pallas_call(functools.partial(layer_kernel, dp_bits), out_shape=[jax.S...]
    reduce_scatter x6 -> x0, waiting for transfers between devices: 144 us -> none  [per_device(): lax.psum_scatter(g.astype(bf16), 'tensor', scatter_dimension=SPLIT[i], ti...]
    psum x1 -> x0, waiting for transfers between devices: 132 us -> none  [per_device(): outs.append(lax.psum(g, 'dp').astype(f32))]
    dot_general x24 -> x0, matrix products: 112 us -> none  [the longest x1 19.7 us: run_slot(): hidden_pre = jnp.dot(first_low, w_up, preferred_element_type=f32) + b_up]
    all_gather x8 -> x0, waiting for transfers between devices: 88.9 us -> none  [the longest x6 88.9 us: per_device(): lax.all_gather(p, 'tensor', axis=SPLIT[i], tiled=True)]
    psum x2 -> x0, blocking collectives: 60 us -> none  [the longest x1 37.8 us: per_device(): outs.append(lax.psum(g, ('dp', 'tensor')))]
    unnamed x2 -> x0, blocking collectives: 18.6 us -> none
    convert_element_type x16 -> x4, other arithmetic: 17.5 us -> 3.5 us  [the longest x2 2 us: per_device(): g_q, g_k, g_v = (g_qkv[:, i].reshape(-1, D).T.astype(F32) for i in range(3))]
  transfers between devices with their start and end apart: 15 -> 0, of which waited for: 11 -> 0; matrix products, arithmetic and copies ran while one was open for 16% -> 0% of each run, Pallas kernels for 0% -> 0%
where the time goes in v2:
time: 287 us; the launch traced here: 286 us
  Pallas kernels  259 us (90%)
  local copies, waits for them, and re-layouts  20.7 us (7%)
  other arithmetic  5.66 us (2%)
    pallas_call x1, Pallas kernels, run_layer(): pl.pallas_call(functools.partial(layer_kernel, dp_bits), out_shape=[jax.S...  259 us

profile of v2, /device:TPU:0, one launch (start us, length us, event | category | flops | bytes accessed | tf_op | source)
XLA Modules:
  0.0 286.5 jit_solution(7329594383179285588)
XLA Ops:
  1.3 0.7 reshape.78
  2.0 0.7 reshape.79
  3.0 0.7 broadcast_in_dim.33
  3.6 0.7 broadcast_in_dim.34
  4.3 0.7 broadcast_in_dim.35
  5.0 0.7 broadcast_in_dim.40
  5.7 0.7 broadcast_in_dim.36
  6.4 0.7 broadcast_in_dim.37
  7.1 0.7 broadcast_in_dim.38
  8.5 2.1 pad_maximum_fusion
  10.6 258.8 %shard_map.314 = (bf16[4,512,768]{2,1,0:T(8,128)(2,1)}, bf16[4,512,768]{2,1,0:T(8,128)(2,1)}, bf16[6,2,2,64,768]{4,3,2,1,0:T(8,128)(2,1)}, bf16[4,2,2,48,768]{4,3,2,1,0:T(8,128)(2,1)}, f32[24,768]{1,0:T(8,128)}) custom-call(bf16[2048,768]{1,0:T(8,128)(2,1)} %tok_hbm.1, bf16[2048,768]{1,0:T(8,128)(2,1)} %cot_hbm.1, s32[4]{0:T(128)} %len_ref.1, ...), custom_call_target="tpu_custom_call" | custom-call | tf_op jit(solution)/shard_map/pallas_call | solution.py:595
  269.4 0.7 slice.67
  270.1 1.6 slice_reduce_fusion
  271.8 0.7 slice.57
  272.6 0.6 reshape.84
  273.8 1.0 slice.62
  274.8 1.2 slice.55
  276.1 0.9 bitcast_convert_fusion
  277.0 0.9 convert_bitcast_fusion.2
  277.9 1.1 convert_bitcast_fusion
  279.0 2.7 fusion
  281.8 1.7 copy.42
  283.5 1.4 copy-done.1
  284.8 1.7 copy.43
  (17 shorter events, 1.7 us)
Async XLA Ops:
  276.1 3.0 %copy-start = (bf16[6,2,2,64,768]{4,3,2,1,0:T(8,128)(2,1)S(1)}, bf16[6,2,2,64,768]{4,3,2,1,0:T(8,128)(2,1)}, u32[]{:S(2)}) copy-start(bf16[6,2,2,64,768]{4,3,2,1,0:T(8,128)(2,1)} %get-tuple-element.26) | copy-start | bytes 7077892
  279.0 2.8 copy-start.2
  281.8 3.0 %copy-start.1 = (bf16[4,512,768]{2,1,0:T(8,128)(2,1)S(1)}, bf16[4,512,768]{2,1,0:T(8,128)(2,1)}, u32[]{:S(2)}) copy-start(bf16[4,512,768]{2,1,0:T(8,128)(2,1)} %get-tuple-element.23) | copy-start | bytes 9437188

commit v3 on v2

--- a/solution.py
+++ b/solution.py
@@ -15,7 +15,27 @@
 BF16 = jnp.bfloat16
 FF_PIECES = 6
 PIECES = 10
-LAG = {2: 1, 3: 3, 4: 4}
+ORDERS = ("zyx", "yzx", "yzx", "xyz", "zyx", "yxz", "xyz", "xyz", "xyz", "xyz")
+AFTER_HEAD = {
+    0: ((1, 2), (2, 2), (0, 2), (3, 2)),
+    1: ((4, 2),),
+    3: ((1, 3), (5, 2)),
+    4: ((0, 3), (6, 2)),
+    5: ((1, 4), (2, 3)),
+    6: ((3, 3),),
+    7: ((5, 3),),
+    8: ((3, 4), (4, 3), (1, 5)),
+    9: ((5, 4), (6, 3), (7, 2)),
+    10: ((0, 4),),
+    11: ((1, 6), (2, 4)),
+}
+AFTER_LAST = (
+    (3, 5), (7, 3), (6, 4), (5, 5), (8, 2), (1, 7), (4, 4), (3, 6),
+    (8, 3), (2, 5), (7, 4), (3, 7), (9, 2), (5, 6), (0, 5), (6, 5),
+    (8, 4), (4, 5), (2, 6), (9, 3), (7, 5), (5, 7), (9, 4), (8, 5),
+    (7, 6), (4, 6), (-1, 0), (0, 6), (6, 6), (8, 6), (9, 5), (2, 7),
+    (4, 7), (7, 7), (6, 7), (9, 6), (8, 7), (0, 7), (9, 7),
+)
 
 
 def flip(value, bit):
@@ -187,18 +207,18 @@
             values = qkv[h, :, 128:192]
 
             def rows(rb, carry):
-                at = block(rb, 128)
+                at = block(rb, 256)
                 scores = dot_nt(qkv[h, at, 0:64], keys) * 0.125 + key_mask
                 top = jnp.max(scores, -1, keepdims=True)
                 expd = jnp.exp(scores - top)
                 total = jnp.sum(expd, -1, keepdims=True)
                 probs = (expd * (1.0 / total)).astype(BF16)
                 ctx[s, at, 64 * j:64 * (j + 1)] = dot_nn(probs, values).astype(BF16)
-                lane = lax.broadcasted_iota(jnp.int32, (128, 128), 1)
+                lane = lax.broadcasted_iota(jnp.int32, (256, 128), 1)
                 lse[s, at] = jnp.where(lane == j, top + jnp.log(total), lse[s, at])
                 return carry
 
-            lax.fori_loop(0, SEQ // 128, rows, 0)
+            lax.fori_loop(0, SEQ // 256, rows, 0, unroll=True)
         return carry
 
     lse[...] = jnp.zeros_like(lse)
@@ -334,67 +354,89 @@
 
     n_exchange = dp_bits - 2
     last = 4 + n_exchange + 2
-    lag = dict(LAG)
-    for s in range(5, last + 1):
-        lag[s] = lag[s - 1] + (2 if s == last else 1)
 
     def att_rows(shard, quarter, count):
         return pl.ds(pl.multiple_of((shard * 4 + quarter) * 48, 48), count)
 
-    def views(ff, p):
-        out = off_ref if ff else oat_ref
-        if ff:
-            return dict(
-                s0=gff.at[p, 1 - c], k0=gff.at[p, c], r0=r0.at[p],
-                s1=gff.at[p, c, 1 - x], k1=gff.at[p, c, x], r1=r1f.at[p],
-                s2=gff.at[p, c, x, 1 - b0], k2=gff.at[p, c, x, b0], r2=r2.at[p],
-                s3=gff.at[p, c, x, b0, 1 - b1], k3=gff.at[p, c, x, b0, b1], r3=r3.at[p],
-                rx=rx, o1=out.at[p, b0, b1], o0=out.at[p, b0],
-            )
-        g = wdn.at[p]
-        r = wup.at[p]
+    mine = {"x": x, "y": b0, "z": b1}
+    peer = {"x": across, "y": dps[0], "z": dps[1]}
+    got_ff = (r0, r1f, r2, r3)
+    all_rows = slice(None)
+
+    def halves(piece, s):
+        if piece < FF_PIECES:
+            place = {axis: mine[axis] for axis in ORDERS[piece][:max(s - 1, 0)]}
+            at = [piece, c] + [place.get(axis, all_rows) for axis in "xyz"]
+            away, keep = list(at), list(at)
+            if s == 0:
+                away[1] = 1 - c
+            else:
+                axis = ORDERS[piece][s - 1]
+                away["xyz".index(axis) + 2] = 1 - mine[axis]
+                keep["xyz".index(axis) + 2] = mine[axis]
+            return gff.at[tuple(away)], gff.at[tuple(keep)], got_ff[s].at[piece]
+        g = wdn.at[piece - FF_PIECES]
+        r = wup.at[piece - FF_PIECES]
         me = 2 * c + x
-        return dict(
-            s0=g.at[att_rows(2 * (1 - c), 0, 384)], k0=g.at[att_rows(2 * c, 0, 384)],
-            r0=r.at[pl.ds(0, 384)],
-            s1=g.at[att_rows(2 * c + 1 - x, 0, 192)], k1=g.at[att_rows(me, 0, 192)],
-            r1=r.at[pl.ds(384, 192)],
-            s2=g.at[att_rows(me, 2 * (1 - b0), 96)], k2=g.at[att_rows(me, 2 * b0, 96)],
-            r2=r.at[pl.ds(576, 96)],
-            s3=g.at[att_rows(me, 2 * b0 + 1 - b1, 48)], k3=g.at[att_rows(me, 2 * b0 + b1, 48)],
-            r3=r.at[pl.ds(672, 48)],
-            rx=rxa, o1=out.at[p, b0, b1], o0=out.at[p, b0],
-        )
-
-    def stage_copy(s, p, ff):
-        v = views(ff, p)
-        base = 0 if ff else FF_PIECES
-        sems = (gs.at[s, base + p], gr.at[s, base + p])
+        if s == 0:
+            return g.at[att_rows(2 * (1 - c), 0, 384)], g.at[att_rows(2 * c, 0, 384)], r.at[pl.ds(0, 384)]
+        if s == 1:
+            return g.at[att_rows(2 * c + 1 - x, 0, 192)], g.at[att_rows(me, 0, 192)], r.at[pl.ds(384, 192)]
+        if s == 2:
+            return (g.at[att_rows(me, 2 * (1 - b0), 96)], g.at[att_rows(me, 2 * b0, 96)],
+                    r.at[pl.ds(576, 96)])
+        return (g.at[att_rows(me, 2 * b0 + 1 - b1, 48)], g.at[att_rows(me, 2 * b0 + b1, 48)],
+                r.at[pl.ds(672, 48)])
+
+    def kept(piece):
+        if piece < FF_PIECES:
+            return gff.at[piece, c, x, b0, b1], rx.at[piece], off_ref.at[piece]
+        own = wdn.at[piece - FF_PIECES, att_rows(2 * c + x, 2 * b0 + b1, 48)]
+        return own, rxa.at[piece - FF_PIECES], oat_ref.at[piece - FF_PIECES]
+
+    def stage_copy(s, piece):
+        sems = (gs.at[s, piece], gr.at[s, piece])
+        order = ORDERS[piece]
         if s < 4:
-            return send(v[f"s{s}"], v[f"r{s}"], *sems, (core, across, dps[0], dps[1])[s])
+            away, _, got = halves(piece, s)
+            return send(away, got, *sems, core if s == 0 else peer[order[s - 1]])
+        own, got, out = kept(piece)
         if s < 4 + n_exchange:
-            k = s - 4
-            return send(v["k3"], v["rx"].at[p, k], *sems, dps[2 + k])
+            return send(own, got.at[s - 4], *sems, dps[s - 2])
+        back = [axis for axis in order if axis != "x"]
         if s == 4 + n_exchange:
-            return send(v["o1"], v["o1"], *sems, dps[1])
-        return send(v["o0"], v["o0"], *sems, dps[0])
-
-    def combine(s, p, ff):
-        v = views(ff, p)
+            part = out.at[b0, b1]
+            return send(part, part, *sems, peer[back[1]])
+        part = out.at[b0] if back[0] == "y" else out.at[:, b1]
+        return send(part, part, *sems, peer[back[0]])
+
+    def combine(s, piece):
         if s < 4:
-            keep, got = v[f"k{s}"], v[f"r{s}"]
+            _, keep, got = halves(piece, s)
             keep[...] = keep[...] + got[...]
         elif s < 4 + n_exchange:
-            k = s - 4
-            total = v["k3"][...] + v["rx"].at[p, k][...]
-            v["o1" if k == n_exchange - 1 else "k3"][...] = total
-
-    def run_stage(s, p, ff):
+            own, got, out = kept(piece)
+            total = own[...] + got[s - 4]
+            if s == 3 + n_exchange:
+                out[b0, b1] = total
+            else:
+                own[...] = total
+
+    def run_stage(s, piece):
         if s > 0:
-            stage_copy(s - 1, p, ff).wait()
-            combine(s - 1, p, ff)
+            stage_copy(s - 1, piece).wait()
+            combine(s - 1, piece)
         if s < last:
-            stage_copy(s, p, ff).start()
+            stage_copy(s, piece).start()
+
+    def late_stage(piece, s):
+        if s < 5:
+            run_stage(s, piece)
+        elif s == 5:
+            for k in range(5, 5 + n_exchange):
+                run_stage(k, piece)
+        else:
+            run_stage(s + n_exchange - 1, piece)
 
     def down_grad(i, carry):
         def shard(s, carry):
@@ -404,11 +446,12 @@
             return carry
 
         lax.fori_loop(0, 4, shard, 0)
-        run_stage(0, i, True)
-
-        @pl.when(i > 0)
-        def _():
-            run_stage(1, i - 1, True)
+        for k in range(3):
+            @pl.when(i == k)
+            def _():
+                run_stage(0, k)
+                if k > 0:
+                    run_stage(1, k - 1)
 
         return carry
 
@@ -417,7 +460,7 @@
     def ffn_back(s, carry):
         @pl.when(s == 1)
         def _():
-            run_stage(1, 2, True)
+            run_stage(1, 2)
             lay_copies[1].wait()
             lay_copies[3].start()
 
@@ -444,11 +487,12 @@
             return carry
 
         lax.fori_loop(0, 4, shard, 0)
-        run_stage(0, 3 + i, True)
-
-        @pl.when(i > 0)
-        def _():
-            run_stage(1, 2 + i, True)
+        for k in range(3):
+            @pl.when(i == k)
+            def _():
+                run_stage(0, 3 + k)
+                if k > 0:
+                    run_stage(1, 2 + k)
 
         return carry
 
@@ -468,7 +512,7 @@
         return carry
 
     lax.fori_loop(0, 4, first_back, 0)
-    run_stage(1, 5, True)
+    run_stage(1, 5)
 
     pl.semaphore_wait(free_sem, len(partners))
 
@@ -481,17 +525,7 @@
         return carry
 
     lax.fori_loop(0, 4, out_back, 0)
-    run_stage(0, 0, False)
-
-    def tail_stages(n):
-        for s in range(last, 1, -1):
-            for ff in (True, False):
-                p = (n - lag[s]) // 3
-                low, high = (0, FF_PIECES) if ff else (FF_PIECES, PIECES)
-
-                @pl.when((n >= lag[s]) & (lax.rem(n + 300 - lag[s], 3) == 0) & (p >= low) & (p < high))
-                def _():
-                    run_stage(s, p - low, ff)
+    run_stage(0, 6)
 
     def head_back(n, carry):
         s = slot_of(lax.rem(n, 4))
@@ -503,10 +537,10 @@
         st[...] = jnp.zeros_like(st)
 
         def rows(rb, carry):
-            at = block(rb, 128)
+            at = block(rb, 256)
             query = qkv[h, at, 0:64]
             gout = gctx[h, at]
-            lane = lax.broadcasted_iota(jnp.int32, (128, 128), 1)
+            lane = lax.broadcasted_iota(jnp.int32, (256, 128), 1)
             norm = jnp.sum(jnp.where(lane == j, lse[s, at], 0.0), -1, keepdims=True)
             probs = jnp.exp(dot_nt(query, keys) * 0.125 + key_mask - norm)
             gprobs = dot_nt(gout, values)
@@ -517,7 +551,7 @@
             st[128:192] = st[128:192] + dot_tn(gout, probs.astype(BF16))
             return carry
 
-        lax.fori_loop(0, SEQ // 128, rows, 0)
+        lax.fori_loop(0, SEQ // 256, rows, 0, unroll=True)
         row = lax.broadcasted_iota(jnp.int32, (192, 1), 0)
         packed = (st[...] * jnp.where(row < 128, 0.125, 1.0)).astype(BF16)
         home = att_rows(2 * lax.rem(s, 2) + s // 2, 0, 192)
@@ -528,23 +562,21 @@
 
         acc[...] = acc[...] + dot_tn(packed, w_rows)
 
-        @pl.when(n == 0)
-        def _():
-            run_stage(1, 0, False)
-
-        @pl.when(lax.rem(n, 4) == 3)
-        def _():
-            run_stage(0, 1 + j, False)
-
-        @pl.when((n > 0) & (lax.rem(n, 4) == 0))
-        def _():
-            run_stage(1, j, False)
-
-        tail_stages(n)
+        for k in range(12):
+            @pl.when(n == k)
+            def _():
+                if k % 4 == 0:
+                    run_stage(1, 6 + k // 4)
+                if k % 4 == 3:
+                    run_stage(0, 7 + k // 4)
+                for piece, s in AFTER_HEAD.get(k, ()):
+                    late_stage(piece, s)
+
         return carry
 
     lax.fori_loop(0, 12, head_back, 0)
     gtok[...] = acc[...].astype(BF16)
+    run_stage(1, 9)
     tok_copies = spread(1, gtok, grad_out)
     for copy in tok_copies[:3]:
         copy.start()
@@ -552,31 +584,30 @@
     def vec_copy(k):
         return send(vec_acc.at[k], vec_in.at[k], vs.at[k], vr.at[k], partners[k])
 
-    vec_copy(0).start()
-    run_stage(1, 3, False)
-    end = max(3 * (PIECES - 1) + lag[last], 13 + 2 * len(partners))
-
-    def drain(n, carry):
-        tail_stages(n)
-        for k in range(len(partners)):
-            @pl.when(n == 14 + 2 * k)
-            def _():
-                vec_copy(k).wait()
-                total = vec_acc[k] + vec_in[k]
-                if k == len(partners) - 1:
-                    vec_out[...] = total
-                else:
-                    vec_acc[k + 1] = total
-                    vec_copy(k + 1).start()
-
-        @pl.when(n == 30)
-        def _():
+    def vec_step(k):
+        if k > 0:
+            vec_copy(k - 1).wait()
+            total = vec_acc[k - 1] + vec_in[k - 1]
+            if k == len(partners):
+                vec_out[...] = total
+                return
+            vec_acc[k] = total
+        vec_copy(k).start()
+
+    vec_step(0)
+    steps = 1
+    for i, (piece, s) in enumerate(AFTER_LAST):
+        if piece < 0:
             tok_copies[1].wait()
             tok_copies[3].start()
-
-        return carry
-
-    lax.fori_loop(12, end + 1, drain, 0)
+        else:
+            late_stage(piece, s)
+        if i % 4 == 3 and steps <= len(partners):
+            vec_step(steps)
+            steps += 1
+    while steps <= len(partners):
+        vec_step(steps)
+        steps += 1
     for copies in (lay_copies, tok_copies):
         copies[0].wait()
         copies[2].wait()

time: 287 us -> 231 us (0.80)
  Pallas kernels: 259 us -> 202 us
    pallas_call x1, Pallas kernels: 259 us -> 202 us  [run_layer(): pl.pallas_call(functools.partial(layer_kernel, dp_bits), out_shape=[jax.S...]
where the time goes in v3:
time: 231 us; the launch traced here: 230 us
  Pallas kernels  202 us (87%)
  local copies, waits for them, and re-layouts  20.7 us (9%)
  other arithmetic  5.66 us (2%)
    pallas_call x1, Pallas kernels, run_layer(): pl.pallas_call(functools.partial(layer_kernel, dp_bits), out_shape=[jax.S...  202 us
    unnamed x8, local copies, waits for them, and re-layouts  4.73 us

profile of v3, /device:TPU:0, one launch (start us, length us, event | category | flops | bytes accessed | tf_op | source)
XLA Modules:
  0.0 230.2 jit_solution(10185079568776464192)
XLA Ops:
  1.3 0.7 reshape.78
  2.0 0.7 reshape.79
  3.0 0.7 broadcast_in_dim.33
  3.6 0.7 broadcast_in_dim.34
  4.3 0.7 broadcast_in_dim.35
  5.0 0.7 broadcast_in_dim.40
  5.7 0.7 broadcast_in_dim.36
  6.4 0.7 broadcast_in_dim.37
  7.1 0.7 broadcast_in_dim.38
  8.5 2.1 pad_maximum_fusion
  10.6 202.5 %shard_map.314 = (bf16[4,512,768]{2,1,0:T(8,128)(2,1)}, bf16[4,512,768]{2,1,0:T(8,128)(2,1)}, bf16[6,2,2,64,768]{4,3,2,1,0:T(8,128)(2,1)}, bf16[4,2,2,48,768]{4,3,2,1,0:T(8,128)(2,1)}, f32[24,768]{1,0:T(8,128)}) custom-call(bf16[2048,768]{1,0:T(8,128)(2,1)} %tok_hbm.1, bf16[2048,768]{1,0:T(8,128)(2,1)} %cot_hbm.1, s32[4]{0:T(128)} %len_ref.1, ...), custom_call_target="tpu_custom_call" | custom-call | tf_op jit(solution)/shard_map/pallas_call | solution.py:626
  213.1 0.7 slice.67
  213.8 1.6 slice_reduce_fusion
  215.5 0.7 slice.57
  216.3 0.6 reshape.84
  217.5 1.0 slice.62
  218.5 1.2 slice.55
  219.8 0.9 bitcast_convert_fusion
  220.7 0.9 convert_bitcast_fusion.2
  221.6 1.1 convert_bitcast_fusion
  222.7 2.7 %fusion = (f32[3,2,2,64,768]{4,3,2,1,0:T(8,128)}, f32[3,2,2,64,768]{4,3,2,1,0:T(8,128)}) fusion(bf16[6,2,2,64,768]{4,3,2,1,0:T(8,128)(2,1)S(1)} %copy-done), kind=kLoop, calls=%fused_computation.14 | loop fusion | bytes 9437184 | tf_op jit(solution)/shard_map/slice | solution.py:707
  225.5 1.7 copy.42
  227.2 1.4 copy-done.1
  228.5 1.7 copy.43
  (17 shorter events, 1.7 us)
Async XLA Ops:
  219.8 3.0 %copy-start = (bf16[6,2,2,64,768]{4,3,2,1,0:T(8,128)(2,1)S(1)}, bf16[6,2,2,64,768]{4,3,2,1,0:T(8,128)(2,1)}, u32[]{:S(2)}) copy-start(bf16[6,2,2,64,768]{4,3,2,1,0:T(8,128)(2,1)} %get-tuple-element.26) | copy-start | bytes 7077892
  222.7 2.8 %copy-start.2 = (bf16[4,512,768]{2,1,0:T(8,128)(2,1)S(1)}, bf16[4,512,768]{2,1,0:T(8,128)(2,1)}, u32[]{:S(2)}) copy-start(bf16[4,512,768]{2,1,0:T(8,128)(2,1)} %get-tuple-element.22) | copy-start | bytes 9437188
  225.5 3.0 %copy-start.1 = (bf16[4,512,768]{2,1,0:T(8,128)(2,1)S(1)}, bf16[4,512,768]{2,1,0:T(8,128)(2,1)}, u32[]{:S(2)}) copy-start(bf16[4,512,768]{2,1,0:T(8,128)(2,1)} %get-tuple-element.23) | copy-start | bytes 9437188

commit v4 on v3

--- a/solution.py
+++ b/solution.py
@@ -15,27 +15,31 @@
 BF16 = jnp.bfloat16
 FF_PIECES = 6
 PIECES = 10
-ORDERS = ("zyx", "yzx", "yzx", "xyz", "zyx", "yxz", "xyz", "xyz", "xyz", "xyz")
+ORDERS = ("yxz", "yzx", "xyz", "zxy", "yzx", "xyz", "xyz", "xyz", "xyz", "xyz")
 AFTER_HEAD = {
-    0: ((1, 2), (2, 2), (0, 2), (3, 2)),
+    0: ((0, 2), (2, 2), (1, 2), (3, 2)),
     1: ((4, 2),),
-    3: ((1, 3), (5, 2)),
-    4: ((0, 3), (6, 2)),
-    5: ((1, 4), (2, 3)),
-    6: ((3, 3),),
-    7: ((5, 3),),
-    8: ((3, 4), (4, 3), (1, 5)),
-    9: ((5, 4), (6, 3), (7, 2)),
-    10: ((0, 4),),
-    11: ((1, 6), (2, 4)),
+    3: ((5, 2),),
+    4: ((2, 3), (1, 3)),
+    6: ((4, 3), (5, 3), (6, 2)),
+    7: ((2, 4),),
+    8: ((0, 3), (5, 4)),
+    9: ((6, 3), (3, 3)),
+    11: ((0, 4), (2, 5)),
 }
 AFTER_LAST = (
-    (3, 5), (7, 3), (6, 4), (5, 5), (8, 2), (1, 7), (4, 4), (3, 6),
-    (8, 3), (2, 5), (7, 4), (3, 7), (9, 2), (5, 6), (0, 5), (6, 5),
-    (8, 4), (4, 5), (2, 6), (9, 3), (7, 5), (5, 7), (9, 4), (8, 5),
-    (7, 6), (4, 6), (-1, 0), (0, 6), (6, 6), (8, 6), (9, 5), (2, 7),
-    (4, 7), (7, 7), (6, 7), (9, 6), (8, 7), (0, 7), (9, 7),
+    (5, 5), (6, 4), (7, 2), (1, 4), (2, 6), (0, 5), (4, 4), (5, 6),
+    (7, 3), (3, 4), (2, 7), (6, 5), (8, 2), (0, 6), (5, 7), (-3, 2),
+    (1, 5), (9, 2), (8, 3), (7, 4), (4, 5), (0, 7), (-3, 3), (6, 6),
+    (1, 6), (8, 4), (9, 3), (3, 5), (-3, 4), (4, 6), (6, 7), (7, 5),
+    (-1, 0), (1, 7), (9, 4), (8, 5), (-3, 5), (7, 6), (4, 7), (8, 6),
+    (9, 5), (3, 6), (7, 7), (9, 6), (8, 7), (-2, 0), (9, 7), (3, 7),
 )
+VIA = (1, 0, 1, 0, 1, 1, 0, 1)
+FETCH_HEAD = {(1, 2): ((0, 0),), (2, 0): ((0, 1), (0, 2)), (2, 2): ((0, 3),), (3, 1): ((1, 1),), (3, 2): ((0, 4),)}
+FETCH_NORM = ((1, 2), (0, 5))
+FETCH_UP = {1: ((1, 3),), 2: ((0, 6), (1, 4)), 3: ((0, 7),)}
+FETCH_DOWN = {0: ((1, 5),)}
 
 
 def flip(value, bit):
@@ -85,7 +89,6 @@
     core = {"tensor": flip(t, 1)}
     across = {"tensor": other}
     dps = [{"dp": flip(d, 1 << k)} for k in range(dp_bits)]
-    beside = dps[0]
     partners = (core, across, *dps)
 
     def send(src, dst, send_sem, recv_sem, device):
@@ -123,11 +126,11 @@
     bias_chip.start()
 
     half_up = up_own.shape[0] // 2
-    half_down = down_own.shape[0] // 2
+    part_down = down_own.shape[0] // 4
     chunks = [
         (qkv_own, wqkv, 0, qkv_own.shape[0]), (out_own, wo, 0, out_own.shape[0]),
         (up_own, wup, 0, half_up), (up_own, wup, half_up, half_up),
-        (down_own, wdn, 0, half_down), (down_own, wdn, half_down, half_down),
+        *[(down_own, wdn, k * part_down, part_down) for k in range(4)],
     ]
 
     def span(base, rows, which):
@@ -135,13 +138,14 @@
 
     hops, chips, relays, mates, lasts = [], [], [], [], []
     for i, (own, full, base, rows) in enumerate(chunks):
-        hops.append(send(own.at[span(base, rows, b0)], full.at[t, span(base, rows, b0)],
+        bit = (b0, b1)[VIA[i]]
+        hops.append(send(own.at[span(base, rows, bit)], full.at[t, span(base, rows, bit)],
                          ws.at[i, 1], wr.at[i, 1], across))
         chips.append(send(own.at[pl.ds(base, rows)], full.at[t, pl.ds(base, rows)],
                           ws.at[i, 0], wr.at[i, 0], core))
-        here = full.at[other, span(base, rows, b0)]
-        there = full.at[other, span(base, rows, 1 - b0)]
-        relays.append(send(here, here, ws.at[i, 2], wr.at[i, 2], beside))
+        here = full.at[other, span(base, rows, bit)]
+        there = full.at[other, span(base, rows, 1 - bit)]
+        relays.append(send(here, here, ws.at[i, 2], wr.at[i, 2], dps[VIA[i]]))
         mates.append(send(here, here, ws.at[i, 3], wr.at[i, 3], core))
         lasts.append(send(there, there, ws.at[i, 4], wr.at[i, 4], core))
         hops[i].start()
@@ -155,6 +159,10 @@
     def from_beside(i):
         relays[i].wait()
         lasts[i].start()
+
+    def fetch(steps):
+        for over_dp, i in steps:
+            (from_beside if over_dp else from_across)(i)
 
     def from_core(i):
         chips[i].wait()
@@ -182,7 +190,6 @@
 
         @pl.when(order == 1)
         def _():
-            from_across(0)
             bias_hop.wait()
             bias_mate.start()
             from_core(0)
@@ -190,13 +197,11 @@
 
         @pl.when(order == 2)
         def _():
-            from_across(1)
             from_beside(0)
             bias_mate.wait()
 
         @pl.when(order == 3)
         def _():
-            from_beside(1)
             from_far(0)
 
         for j in range(3):
@@ -207,24 +212,28 @@
             values = qkv[h, :, 128:192]
 
             def rows(rb, carry):
-                at = block(rb, 256)
+                at = block(rb, 512)
                 scores = dot_nt(qkv[h, at, 0:64], keys) * 0.125 + key_mask
                 top = jnp.max(scores, -1, keepdims=True)
                 expd = jnp.exp(scores - top)
                 total = jnp.sum(expd, -1, keepdims=True)
                 probs = (expd * (1.0 / total)).astype(BF16)
                 ctx[s, at, 64 * j:64 * (j + 1)] = dot_nn(probs, values).astype(BF16)
-                lane = lax.broadcasted_iota(jnp.int32, (256, 128), 1)
+                lane = lax.broadcasted_iota(jnp.int32, (512, 128), 1)
                 lse[s, at] = jnp.where(lane == j, top + jnp.log(total), lse[s, at])
                 return carry
 
-            lax.fori_loop(0, SEQ // 256, rows, 0, unroll=True)
+            lax.fori_loop(0, SEQ // 512, rows, 0, unroll=True)
+            for o in range(4):
+                if (o, j) in FETCH_HEAD:
+                    @pl.when(order == o)
+                    def _():
+                        fetch(FETCH_HEAD[(o, j)])
         return carry
 
     lse[...] = jnp.zeros_like(lse)
     lax.fori_loop(0, 4, attend, 0)
 
-    from_across(2)
     from_core(1)
     from_far(1)
     loads[2].wait()
@@ -248,7 +257,7 @@
 
     lax.fori_loop(0, 4, project, 0)
 
-    from_across(3)
+    fetch(FETCH_NORM)
     loads[3].wait()
 
     def raise_up(order, carry):
@@ -256,14 +265,8 @@
 
         @pl.when(order == 1)
         def _():
-            from_beside(2)
             from_core(2)
             from_core(3)
-
-        @pl.when(order == 2)
-        def _():
-            from_across(4)
-            from_beside(3)
 
         @pl.when(order == 3)
         def _():
@@ -280,11 +283,13 @@
             return carry
 
         lax.fori_loop(0, 4, rows, 0)
+        for o, steps in FETCH_UP.items():
+            @pl.when(order == o)
+            def _():
+                fetch(steps)
         return carry
 
     lax.fori_loop(0, 4, raise_up, 0)
-    from_across(5)
-    from_beside(4)
     loads[4].wait()
 
     def bring_down(order, carry):
@@ -292,17 +297,18 @@
 
         @pl.when(order == 1)
         def _():
-            from_core(4)
-            from_core(5)
+            for i in range(4, 8):
+                from_core(i)
 
         @pl.when(order == 2)
         def _():
-            from_beside(5)
+            from_beside(6)
+            from_beside(7)
 
         @pl.when(order == 3)
         def _():
-            from_far(4)
-            from_far(5)
+            for i in range(4, 8):
+                from_far(i)
 
         def rows(rb, carry):
             at = block(rb, 256)
@@ -310,6 +316,10 @@
             return carry
 
         lax.fori_loop(0, 2, rows, 0)
+        for o, steps in FETCH_DOWN.items():
+            @pl.when(order == o)
+            def _():
+                fetch(steps)
         return carry
 
     lax.fori_loop(0, 4, bring_down, 0)
@@ -349,8 +359,8 @@
         )
 
     lay_copies = spread(0, lay, layer_out)
-    for copy in lay_copies[:3]:
-        copy.start()
+    lay_copies[0].start()
+    lay_copies[2].start()
 
     n_exchange = dp_bits - 2
     last = 4 + n_exchange + 2
@@ -461,8 +471,6 @@
         @pl.when(s == 1)
         def _():
             run_stage(1, 2)
-            lay_copies[1].wait()
-            lay_copies[3].start()
 
         def rows(rb, carry):
             at = block(rb, 256)
@@ -537,10 +545,10 @@
         st[...] = jnp.zeros_like(st)
 
         def rows(rb, carry):
-            at = block(rb, 256)
+            at = block(rb, 512)
             query = qkv[h, at, 0:64]
             gout = gctx[h, at]
-            lane = lax.broadcasted_iota(jnp.int32, (256, 128), 1)
+            lane = lax.broadcasted_iota(jnp.int32, (512, 128), 1)
             norm = jnp.sum(jnp.where(lane == j, lse[s, at], 0.0), -1, keepdims=True)
             probs = jnp.exp(dot_nt(query, keys) * 0.125 + key_mask - norm)
             gprobs = dot_nt(gout, values)
@@ -551,7 +559,7 @@
             st[128:192] = st[128:192] + dot_tn(gout, probs.astype(BF16))
             return carry
 
-        lax.fori_loop(0, SEQ // 256, rows, 0, unroll=True)
+        lax.fori_loop(0, SEQ // 512, rows, 0, unroll=True)
         row = lax.broadcasted_iota(jnp.int32, (192, 1), 0)
         packed = (st[...] * jnp.where(row < 128, 0.125, 1.0)).astype(BF16)
         home = att_rows(2 * lax.rem(s, 2) + s // 2, 0, 192)
@@ -575,12 +583,6 @@
         return carry
 
     lax.fori_loop(0, 12, head_back, 0)
-    gtok[...] = acc[...].astype(BF16)
-    run_stage(1, 9)
-    tok_copies = spread(1, gtok, grad_out)
-    for copy in tok_copies[:3]:
-        copy.start()
-
     def vec_copy(k):
         return send(vec_acc.at[k], vec_in.at[k], vs.at[k], vr.at[k], partners[k])
 
@@ -595,19 +597,22 @@
         vec_copy(k).start()
 
     vec_step(0)
-    steps = 1
-    for i, (piece, s) in enumerate(AFTER_LAST):
-        if piece < 0:
-            tok_copies[1].wait()
-            tok_copies[3].start()
+    gtok[...] = acc[...].astype(BF16)
+    run_stage(1, 9)
+    vec_step(1)
+    tok_copies = spread(1, gtok, grad_out)
+    for copy in (*tok_copies[:3], lay_copies[1]):
+        copy.start()
+    for piece, s in AFTER_LAST:
+        if piece == -3:
+            for k in (s,) if s < 5 else range(5, len(partners) + 1):
+                vec_step(k)
+        elif piece < 0:
+            copies = tok_copies if piece == -1 else lay_copies
+            copies[1].wait()
+            copies[3].start()
         else:
             late_stage(piece, s)
-        if i % 4 == 3 and steps <= len(partners):
-            vec_step(steps)
-            steps += 1
-    while steps <= len(partners):
-        vec_step(steps)
-        steps += 1
     for copies in (lay_copies, tok_copies):
         copies[0].wait()
         copies[2].wait()
@@ -662,7 +667,7 @@
             pltpu.VMEM((4, n_exchange, 48, D), BF16),
             pltpu.VMEM((links, 24, D), F32),
             pltpu.VMEM((links, 24, D), F32),
-            dma((6, 5)), dma((6, 5)),
+            dma((8, 5)), dma((8, 5)),
             dma((stages, PIECES)), dma((stages, PIECES)),
             dma((links,)), dma((links,)),
             dma((2, 3)), dma((2, 3)),

time: 231 us -> 196 us (0.85)
  Pallas kernels: 202 us -> 167 us
    pallas_call x1, Pallas kernels: 202 us -> 167 us  [run_layer(): pl.pallas_call(functools.partial(layer_kernel, dp_bits), out_shape=[jax.S...]
where the time goes in v4:
time: 196 us; the launch traced here: 195 us
  Pallas kernels  167 us (85%)
  local copies, waits for them, and re-layouts  20.7 us (11%)
  other arithmetic  5.66 us (3%)
    pallas_call x1, Pallas kernels, run_layer(): pl.pallas_call(functools.partial(layer_kernel, dp_bits), out_shape=[jax.S...  167 us
    unnamed x8, local copies, waits for them, and re-layouts  4.73 us
    broadcast_in_dim x6, local copies, waits for them, and re-layouts, per_device(): v[None]  4.11 us

profile of v4, /device:TPU:0, one launch (start us, length us, event | category | flops | bytes accessed | tf_op | source)
XLA Modules:
  0.0 195.0 jit_solution(6996317817125273361)
XLA Ops:
  1.3 0.7 reshape.78
  2.0 0.7 reshape.79
  3.0 0.7 broadcast_in_dim.33
  3.6 0.7 broadcast_in_dim.34
  4.3 0.7 broadcast_in_dim.35
  5.0 0.7 broadcast_in_dim.40
  5.7 0.7 broadcast_in_dim.36
  6.4 0.7 broadcast_in_dim.37
  7.1 0.7 broadcast_in_dim.38
  8.5 2.1 %pad_maximum_fusion = bf16[768,3,3,64]{0,3,1,2:T(8,128)(2,1)} fusion(bf16[768,1,3,64]{0,3,1,2:T(8,128)(2,1)} %bitcast.41, bf16[768,1,3,64]{0,3,1,2:T(8,128)(2,1)} %bitcast.42, bf16[768,1,3,64]{0,3,1,2:T(8,128)(2,1)} %bitcast.43), kind=kLoop, calls=%fused_computation | loop fusion | flops 884736 | bytes 1769472 | tf_op jit(solution)/shard_map/stack | solution.py:689
  10.6 167.3 %shard_map.314 = (bf16[4,512,768]{2,1,0:T(8,128)(2,1)}, bf16[4,512,768]{2,1,0:T(8,128)(2,1)}, bf16[6,2,2,64,768]{4,3,2,1,0:T(8,128)(2,1)}, bf16[4,2,2,48,768]{4,3,2,1,0:T(8,128)(2,1)}, f32[24,768]{1,0:T(8,128)}) custom-call(bf16[2048,768]{1,0:T(8,128)(2,1)} %tok_hbm.1, bf16[2048,768]{1,0:T(8,128)(2,1)} %cot_hbm.1, s32[4]{0:T(128)} %len_ref.1, ...), custom_call_target="tpu_custom_call" | custom-call | tf_op jit(solution)/shard_map/pallas_call | solution.py:631
  177.9 0.7 slice.67
  178.6 1.6 slice_reduce_fusion
  180.3 0.7 slice.57
  181.1 0.6 reshape.84
  182.4 1.0 slice.62
  183.3 1.2 slice.55
  184.7 0.9 bitcast_convert_fusion
  185.5 0.9 convert_bitcast_fusion.2
  186.4 1.1 convert_bitcast_fusion
  187.5 2.7 %fusion = (f32[3,2,2,64,768]{4,3,2,1,0:T(8,128)}, f32[3,2,2,64,768]{4,3,2,1,0:T(8,128)}) fusion(bf16[6,2,2,64,768]{4,3,2,1,0:T(8,128)(2,1)S(1)} %copy-done), kind=kLoop, calls=%fused_computation.14 | loop fusion | bytes 9437184 | tf_op jit(solution)/shard_map/slice | solution.py:712
  190.3 1.7 copy.42
  192.0 1.4 copy-done.1
  193.4 1.7 copy.43
  (17 shorter events, 1.7 us)
Async XLA Ops:
  184.6 3.0 %copy-start = (bf16[6,2,2,64,768]{4,3,2,1,0:T(8,128)(2,1)S(1)}, bf16[6,2,2,64,768]{4,3,2,1,0:T(8,128)(2,1)}, u32[]{:S(2)}) copy-start(bf16[6,2,2,64,768]{4,3,2,1,0:T(8,128)(2,1)} %get-tuple-element.26) | copy-start | bytes 7077892
  187.5 2.8 %copy-start.2 = (bf16[4,512,768]{2,1,0:T(8,128)(2,1)S(1)}, bf16[4,512,768]{2,1,0:T(8,128)(2,1)}, u32[]{:S(2)}) copy-start(bf16[4,512,768]{2,1,0:T(8,128)(2,1)} %get-tuple-element.22) | copy-start | bytes 9437188
  190.3 3.0 %copy-start.1 = (bf16[4,512,768]{2,1,0:T(8,128)(2,1)S(1)}, bf16[4,512,768]{2,1,0:T(8,128)(2,1)}, u32[]{:S(2)}) copy-start(bf16[4,512,768]{2,1,0:T(8,128)(2,1)} %get-tuple-element.23) | copy-start | bytes 9437188

commit v5 on v4

--- a/solution.py
+++ b/solution.py
@@ -75,10 +75,12 @@
 
 
 def layer_kernel(dp_bits, tok_hbm, cot_hbm, len_ref, cnt_ref, qkv_own, out_own, up_own, down_own,
-                 rows_ref, layer_out, grad_out, off_ref, oat_ref, vec_out,
+                 *refs):
+    vectors, refs = refs[:9], refs[9:]
+    (layer_out, grad_out, off_ref, oat_ref, vec_out,
                  wqkv, wo, wup, wdn, bias, tok, cot, qkv, ctx, lse, n1, r1, flow, hid, gd, gr2,
                  glow, acc, gctx, st, stage_rows, gff, r0, r1f, r2, r3, rx, rxa, vec_acc, vec_in,
-                 ws, wr, gs, gr, vs, vr, os, orr, bs, br, ls, free_sem):
+                 ws, wr, gs, gr, vs, vr, os, orr, bs, br, ls, free_sem, rows_ref) = refs
     t = lax.axis_index("tensor")
     d = lax.axis_index("dp")
     c = lax.rem(t, 2)
@@ -112,6 +114,11 @@
     ]
     for load in loads:
         load.start()
+    rows_ref[...] = jnp.zeros_like(rows_ref)
+    for i, ref in enumerate(vectors):
+        row = i if i < 6 else i + 2
+        width = ref.shape[0]
+        rows_ref[row:row + 1, 0:width] = ref[...].astype(F32).reshape(1, width)
     bias[t] = rows_ref[8:16]
     barrier = pltpu.get_barrier_semaphore()
     for device in partners:
@@ -207,7 +214,11 @@
         for j in range(3):
             h = 3 * s + j
             w_rows = wqkv[s, 192 * j:192 * (j + 1)]
-            qkv[h] = (dot_nt(tok[...], w_rows) + bias[s, 1 + j:2 + j, 0:192]).astype(BF16)
+            lanes = slice(64 * j, 64 * (j + 1))
+            packed = dot_nt(tok[...], w_rows)
+            qkv[h, :, 0:64] = (packed[:, 0:64] + bias[s, 1:2, lanes]).astype(BF16)
+            qkv[h, :, 64:128] = packed[:, 64:128].astype(BF16)
+            qkv[h, :, 128:192] = (packed[:, 128:192] + bias[s, 2:3, lanes]).astype(BF16)
             keys = qkv[h, :, 64:128]
             values = qkv[h, :, 128:192]
 
@@ -619,7 +630,7 @@
         copies[3].wait()
 
 
-def run_layer(dp, tokens, cotangent, key_lengths, slot_counts, shards, rows):
+def run_layer(dp, tokens, cotangent, key_lengths, slot_counts, shards, vectors):
     dp_bits = dp.bit_length() - 1
     n_exchange = dp_bits - 2
     stages = 4 + n_exchange + 2
@@ -637,7 +648,7 @@
             jax.ShapeDtypeStruct((4, 2, 2, 48, D), BF16),
             jax.ShapeDtypeStruct((24, D), F32),
         ],
-        in_specs=[hbm, hbm, smem, smem] + [hbm] * 4 + [vmem],
+        in_specs=[hbm, hbm, smem, smem] + [hbm] * 4 + [vmem] * len(vectors),
         out_specs=[hbm] * 2 + [vmem] * 3,
         scratch_shapes=[
             *[pltpu.VMEM((4, *s.shape), BF16) for s in shards],
@@ -674,11 +685,51 @@
             dma((3,)), dma((3,)),
             dma((8,)),
             pltpu.SemaphoreType.REGULAR,
+            pltpu.VMEM((16, D), F32),
         ],
         compiler_params=pltpu.CompilerParams(
             collective_id=0, has_side_effects=True, vmem_limit_bytes=67043328
         ),
-    )(tokens, cotangent, key_lengths, slot_counts, *shards, rows)
+    )(tokens, cotangent, key_lengths, slot_counts, *shards, *vectors)
+
+
+def finish_kernel(layer, grad, ff, att, vec, layer_out, grad_out, down, up, out, g_q, g_k, g_v, *sums):
+    layer_out[...] = layer[0]
+    grad_out[...] = grad[0]
+    down[...] = ff[0].astype(F32)
+    up[...] = ff[1].astype(F32)
+
+    @pl.when(pl.program_id(0) == 0)
+    def _():
+        t = lax.axis_index("tensor")
+        out[...] = att[0].astype(F32)
+        for i, ref in enumerate((g_q, g_k, g_v)):
+            for j in range(3):
+                ref[64 * j:64 * (j + 1)] = att[1 + j, 64 * i:64 * (i + 1)].astype(F32)
+        for i, ref in enumerate(sums):
+            row = vec[i:i + 1] if i < 6 else vec[pl.ds(8 + t, 1)]
+            ref[...] = row.reshape(D)
+
+
+def finish(layer, grad, ff, att, vec):
+    rows, part = 4 * SEQ, ff.shape[1] // 4
+    shard = jax.ShapeDtypeStruct(att.shape[1:], F32)
+    square = jax.ShapeDtypeStruct(ff.shape[1:], F32)
+    line = jax.ShapeDtypeStruct((D,), F32)
+    slot_in = pl.BlockSpec((1, SEQ, D), lambda i: (i, 0, 0))
+    slot_out = pl.BlockSpec((SEQ, D), lambda i: (i, 0))
+    part_out = pl.BlockSpec((part, D), lambda i: (i, 0))
+    return pl.pallas_call(
+        finish_kernel,
+        grid=(4,),
+        out_shape=[jax.ShapeDtypeStruct((rows, D), BF16)] * 2 + [square] * 2 + [shard] * 4 + [line] * 7,
+        in_specs=[slot_in, slot_in, pl.BlockSpec((2, part, D), lambda i: (0, i, 0)),
+                  pl.BlockSpec(att.shape, lambda i: (0, 0, 0)), pl.BlockSpec(vec.shape, lambda i: (0, 0))],
+        out_specs=[slot_out, slot_out, part_out, part_out]
+        + [pl.BlockSpec(shard.shape, lambda i: (0, 0))] * 4
+        + [pl.BlockSpec((D,), lambda i: (0,))] * 7,
+        compiler_params=pltpu.CompilerParams(vmem_limit_bytes=67043328),
+    )(layer, grad, ff, att, vec)
 
 
 def per_device(dp, tokens, cotangent, key_lengths, slot_counts, *params):
@@ -688,28 +739,17 @@
     heads = w_query.shape[1] // HD
     qkv = jnp.stack([w.reshape(D, heads, HD) for w in (w_query, w_key, w_value)], 1)
     qkv = qkv.transpose(2, 1, 3, 0).reshape(-1, D)
-    q_bias = b_query.reshape(heads, HD)
-    v_bias = b_value.reshape(heads, HD)
-    qkv_bias = jnp.concatenate(
-        (q_bias, jnp.zeros_like(q_bias), v_bias, jnp.zeros((heads, D - 3 * HD), BF16)), 1
+    vectors = (b_out, attn_gain, attn_shift, b_down, ffn_gain, ffn_shift, b_up, b_query, b_value)
+    layer, grad, off, oat, vec = run_layer(
+        dp, tokens, cotangent, key_lengths, slot_counts, (qkv, w_out, w_up, w_down), vectors
     )
-    rows = jnp.concatenate(
-        [v[None] for v in (b_out, attn_gain, attn_shift, b_down, ffn_gain, ffn_shift)]
-        + [jnp.zeros((2, D), BF16), b_up[None], qkv_bias, jnp.zeros((4, D), BF16)], 0
-    ).astype(F32)
-    layer, grad, off, oat, vec = run_layer(
-        dp, tokens, cotangent, key_lengths, slot_counts, (qkv, w_out, w_up, w_down), rows
+    layer, grad, g_down, g_up, g_out, g_q, g_k, g_v, *sums = finish(
+        layer, grad, off.reshape(2, -1, D), oat.reshape(4, -1, D), vec
     )
-    off = off.reshape(2, -1, D).astype(F32)
-    oat = oat.reshape(4, -1, D)
-    g_out = oat[0].astype(F32)
-    g_qkv = oat[1:].reshape(heads, 3, HD, D)
-    g_q, g_k, g_v = (g_qkv[:, i].reshape(-1, D).T.astype(F32) for i in range(3))
     b_qkv = lax.dynamic_slice_in_dim(vec[12:, :3 * HD], slot * heads, heads)
-    gb_up = lax.dynamic_slice_in_dim(vec[8:12], slot, 1)[0]
-    return (layer.reshape(-1, D), grad.reshape(-1, D),
-            g_q, b_qkv[:, :HD].reshape(-1), g_k, g_v, b_qkv[:, 2 * HD:].reshape(-1), g_out,
-            vec[3], vec[4], vec[5], off[1], gb_up, off[0], vec[0], vec[1], vec[2])
+    return (layer, grad, g_q.T, b_qkv[:, :HD].reshape(-1), g_k.T, g_v.T,
+            b_qkv[:, 2 * HD:].reshape(-1), g_out, sums[3], sums[4], sums[5], g_up, sums[6],
+            g_down, sums[0], sums[1], sums[2])
 
 
 def solution(mesh):

time: 196 us -> 182 us (0.929)
  local copies, waits for them, and re-layouts: 20.7 us -> 2.08 us
  Pallas kernels: 167 us -> 176 us
  other arithmetic: 5.66 us -> 2.15 us
    pallas_call x0 -> x1, Pallas kernels: none -> 9.01 us  [finish(): pl.pallas_call(finish_kernel, grid=(4,), out_shape=[jax.ShapeDtypeStruct(...]
    slice x6 -> x0, local copies, waits for them, and re-layouts: 7.4 us -> none  [the longest x1 2.75 us: per_device(): off[0]]
    broadcast_in_dim x11 -> x0, local copies, waits for them, and re-layouts: 4.81 us -> none  [the longest x6 4.11 us: per_device(): v[None]]
    unnamed x8 -> x0, local copies, waits for them, and re-layouts: 4.73 us -> none
    convert_element_type x4 -> x0, other arithmetic: 3.5 us -> none  [the longest x2 2 us: per_device(): g_q, g_k, g_v = (g_qkv[:, i].reshape(-1, D).T.astype(F32) for i in range(3))]
where the time goes in v5:
time: 182 us
  Pallas kernels  176 us (97%)
  other arithmetic  2.15 us (1%)
  local copies, waits for them, and re-layouts  2.08 us (1%)
    pallas_call x1, Pallas kernels, run_layer(): pl.pallas_call(functools.partial(layer_kernel, dp_bits), out_shape=[jax.S...  167 us
    pallas_call x1, Pallas kernels, finish(): pl.pallas_call(finish_kernel, grid=(4,), out_shape=[jax.ShapeDtypeStruct(...  9.01 us

profile of v5, /device:TPU:0, one launch (start us, length us, event | category | flops | bytes accessed | tf_op | source)
XLA Modules:
  0.0 181.9 jit_solution(12585173337773623195)
XLA Ops:
  0.7 2.2 %pad_maximum_fusion = bf16[768,3,3,64]{0,3,1,2:T(8,128)(2,1)} fusion(bf16[768,1,3,64]{0,3,1,2:T(8,128)(2,1)} %bitcast.20, bf16[768,1,3,64]{0,3,1,2:T(8,128)(2,1)} %bitcast.21, bf16[768,1,3,64]{0,3,1,2:T(8,128)(2,1)} %bitcast.22), kind=kLoop, calls=%fused_computation | loop fusion | flops 884736 | bytes 1769472 | tf_op jit(solution)/shard_map/stack | solution.py:740
  3.5 167.4 %shard_map.314 = (bf16[4,512,768]{2,1,0:T(8,128)(2,1)}, bf16[4,512,768]{2,1,0:T(8,128)(2,1)}, bf16[6,2,2,64,768]{4,3,2,1,0:T(8,128)(2,1)}, bf16[4,2,2,48,768]{4,3,2,1,0:T(8,128)(2,1)}, f32[24,768]{1,0:T(8,128)}) custom-call(bf16[2048,768]{1,0:T(8,128)(2,1)} %tok_hbm.1, bf16[2048,768]{1,0:T(8,128)(2,1)} %cot_hbm.1, s32[4]{0:T(128)} %len_ref.1, ...), custom_call_target="tpu_custom_call" | custom-call | tf_op jit(solution)/shard_map/pallas_call | solution.py:642
  170.8 9.0 %shard_map.315 = (bf16[2048,768]{1,0:T(8,128)(2,1)}, bf16[2048,768]{1,0:T(8,128)(2,1)}, f32[768,768]{1,0:T(8,128)}, f32[768,768]{1,0:T(8,128)}, f32[192,768]{1,0...) custom-call(bf16[4,512,768]{2,1,0:T(8,128)(2,1)} %get-tuple-element., ...), custom_call_target="tpu_custom_call" | custom-call | tf_op jit(solution)/shard_map/pallas_call | solution.py:722
  179.8 0.7 slice.9
  180.6 0.1 fusion
  180.6 0.6 reshape.52
  181.3 0.6 reshape.53

commit v6 on v5

--- a/solution.py
+++ b/solution.py
@@ -15,25 +15,25 @@
 BF16 = jnp.bfloat16
 FF_PIECES = 6
 PIECES = 10
-ORDERS = ("yxz", "yzx", "xyz", "zxy", "yzx", "xyz", "xyz", "xyz", "xyz", "xyz")
+ORDERS = ("xyz", "yxz", "zxy", "xyz", "zyx", "yzx", "xyz", "xyz", "xyz", "xyz")
 AFTER_HEAD = {
-    0: ((0, 2), (2, 2), (1, 2), (3, 2)),
+    0: ((1, 2), (3, 2), (0, 2), (2, 2)),
     1: ((4, 2),),
     3: ((5, 2),),
-    4: ((2, 3), (1, 3)),
-    6: ((4, 3), (5, 3), (6, 2)),
-    7: ((2, 4),),
-    8: ((0, 3), (5, 4)),
-    9: ((6, 3), (3, 3)),
-    11: ((0, 4), (2, 5)),
+    4: ((6, 2), (3, 3)),
+    6: ((1, 3), (5, 3)),
+    7: ((3, 4), (0, 3)),
+    8: ((1, 4), (4, 3), (2, 3)),
+    10: ((6, 3), (0, 4)),
+    11: ((3, 5), (7, 2), (2, 4)),
 }
 AFTER_LAST = (
-    (5, 5), (6, 4), (7, 2), (1, 4), (2, 6), (0, 5), (4, 4), (5, 6),
-    (7, 3), (3, 4), (2, 7), (6, 5), (8, 2), (0, 6), (5, 7), (-3, 2),
-    (1, 5), (9, 2), (8, 3), (7, 4), (4, 5), (0, 7), (-3, 3), (6, 6),
-    (1, 6), (8, 4), (9, 3), (3, 5), (-3, 4), (4, 6), (6, 7), (7, 5),
-    (-1, 0), (1, 7), (9, 4), (8, 5), (-3, 5), (7, 6), (4, 7), (8, 6),
-    (9, 5), (3, 6), (7, 7), (9, 6), (8, 7), (-2, 0), (9, 7), (3, 7),
+    (3, 6), (1, 5), (6, 4), (5, 4), (3, 7), (1, 6), (0, 5), (4, 4),
+    (7, 3), (8, 2), (6, 5), (-3, 2), (9, 2), (1, 7), (0, 6), (5, 5),
+    (-3, 3), (6, 6), (4, 5), (7, 4), (8, 3), (-3, 4), (9, 3), (5, 6),
+    (2, 5), (0, 7), (8, 4), (7, 5), (-3, 5), (-1, 0), (6, 7), (9, 4),
+    (4, 6), (7, 6), (8, 5), (5, 7), (9, 5), (4, 7), (8, 6), (7, 7),
+    (9, 6), (2, 6), (8, 7), (-2, 0), (9, 7), (2, 7),
 )
 VIA = (1, 0, 1, 0, 1, 1, 0, 1)
 FETCH_HEAD = {(1, 2): ((0, 0),), (2, 0): ((0, 1), (0, 2)), (2, 2): ((0, 3),), (3, 1): ((1, 1),), (3, 2): ((0, 4),)}

time: 182 us -> 178 us (0.978)
  Pallas kernels: 176 us -> 173 us
    pallas_call x1, Pallas kernels: 167 us -> 164 us  [run_layer(): pl.pallas_call(functools.partial(layer_kernel, dp_bits), out_shape=[jax.S...]
where the time goes in v6:
time: 178 us
  Pallas kernels  173 us (97%)
  other arithmetic  2.15 us (1%)
  local copies, waits for them, and re-layouts  2.08 us (1%)
    pallas_call x1, Pallas kernels, run_layer(): pl.pallas_call(functools.partial(layer_kernel, dp_bits), out_shape=[jax.S...  164 us
    pallas_call x1, Pallas kernels, finish(): pl.pallas_call(finish_kernel, grid=(4,), out_shape=[jax.ShapeDtypeStruct(...  9.01 us

profile of v6, /device:TPU:0, one launch (start us, length us, event | category | flops | bytes accessed | tf_op | source)
XLA Modules:
  0.0 178.1 jit_solution(5988795331334313776)
XLA Ops:
  0.7 2.2 %pad_maximum_fusion = bf16[768,3,3,64]{0,3,1,2:T(8,128)(2,1)} fusion(bf16[768,1,3,64]{0,3,1,2:T(8,128)(2,1)} %bitcast.20, bf16[768,1,3,64]{0,3,1,2:T(8,128)(2,1)} %bitcast.21, bf16[768,1,3,64]{0,3,1,2:T(8,128)(2,1)} %bitcast.22), kind=kLoop, calls=%fused_computation | loop fusion | flops 884736 | bytes 1769472 | tf_op jit(solution)/shard_map/stack | solution.py:740
  3.5 163.5 %shard_map.314 = (bf16[4,512,768]{2,1,0:T(8,128)(2,1)}, bf16[4,512,768]{2,1,0:T(8,128)(2,1)}, bf16[6,2,2,64,768]{4,3,2,1,0:T(8,128)(2,1)}, bf16[4,2,2,48,768]{4,3,2,1,0:T(8,128)(2,1)}, f32[24,768]{1,0:T(8,128)}) custom-call(bf16[2048,768]{1,0:T(8,128)(2,1)} %tok_hbm.1, bf16[2048,768]{1,0:T(8,128)(2,1)} %cot_hbm.1, s32[4]{0:T(128)} %len_ref.1, ...), custom_call_target="tpu_custom_call" | custom-call | tf_op jit(solution)/shard_map/pallas_call | solution.py:642
  167.0 9.0 %shard_map.315 = (bf16[2048,768]{1,0:T(8,128)(2,1)}, bf16[2048,768]{1,0:T(8,128)(2,1)}, f32[768,768]{1,0:T(8,128)}, f32[768,768]{1,0:T(8,128)}, f32[192,768]{1,0...) custom-call(bf16[4,512,768]{2,1,0:T(8,128)(2,1)} %get-tuple-element., ...), custom_call_target="tpu_custom_call" | custom-call | tf_op jit(solution)/shard_map/pallas_call | solution.py:722
  176.0 0.7 slice.9
  176.7 0.1 fusion
  176.8 0.6 reshape.52
  177.4 0.6 reshape.53
